TPU v7x, 128 devices: a whole 4x4x4 slice. The times are simulated.
128 devices in a mesh: dp: 16 (over x, y), tensor: 8 (over z, core).
Axes of the slice: x: 4, y: 4, z: 4, core: 2. Of those that a mesh axis runs over, the one named last changes fastest.
Arguments:
- hidden_rows: bfloat16 [256, 32, 8192], P('tensor', 'dp'), may hold values from -6 to 6
- norm_gain: float32 [8192], replicated, may hold values from 0.1 to 1.9
- w_query: bfloat16 [8192, 4096], P(None, 'tensor'), may hold values from -0.0625 to 0.0625
- w_key: bfloat16 [8192, 1024], P(None, 'tensor'), may hold values from -0.0625 to 0.0625
- w_value: bfloat16 [8192, 1024], P(None, 'tensor'), may hold values from -0.0625 to 0.0625
- w_out: bfloat16 [4096, 8192], P('tensor'), may hold values from -1.5 to 1.5
- cache_keys: bfloat16 [32, 2048, 1024], P('dp', None, 'tensor'), may hold values from -6 to 6
- cache_values: bfloat16 [32, 2048, 1024], P('dp', None, 'tensor'), may hold values from -6 to 6
- slot_of_request: int32 [32], replicated, may hold values from 0 to 31, as said below
- span_length: int32 [32], replicated, may hold values from 1 to 256, as said below
- prefix_length: int32 [32], replicated, may hold values from 1 to 2048, as said below
Outputs:
- attention_out: bfloat16 [256, 32, 8192], P('tensor', 'dp')
Inputs may be any that keep to these rules, and one draw needn't show every extreme that they name: `slot_of_request`: a permutation of the slots 0 to 31; slot i lies on dp index i // 2, request r starts on dp index r // 2; there are 2 distinct numbers m, one of them 1, the same for every dp index, such that the 2 requests of dp index i have their slots on the dp indices i XOR m, one on each. `span_length`: some request uses all 256 new positions. `prefix_length`: some request has all 2048 cached positions.
All inputs are finite; a program needn't handle non-finite values.
Results may differ from a plain program's by a relative error of at most 0.019.
Values may be sent and summed in bfloat16 or wider, within the bound.
A program may use at most 128 MiB of HBM per device.

v0:
```python
import jax
import jax.numpy as jnp
from jax import lax
from jax.sharding import PartitionSpec as P

HD = 128


rope_base = 500000.0
norm_eps = 1e-05
masked = -1e30


def rotate(values, position):
    head_width = values.shape[-1]
    half_width = head_width // 2
    frequency = rope_base ** (-(jnp.arange(half_width, dtype=jnp.float32) * 2.0 / head_width))
    angles = position[..., None, None] * frequency
    cosine = jnp.cos(angles)
    sine_part = jnp.sin(angles)
    front_half = values[..., :half_width]
    back_half = values[..., half_width:]
    return jnp.concatenate(
        [front_half * cosine - back_half * sine_part, back_half * cosine + front_half * sine_part],
        axis=-1,
    )


def normalize(hidden_rows, norm_gain):
    floats = hidden_rows.astype(jnp.float32)
    return (
        floats * lax.rsqrt(jnp.mean(floats * floats, axis=-1, keepdims=True) + norm_eps) * norm_gain
    ).astype(jnp.bfloat16)


def project_group(normed, prefix_here, w_query, w_key, w_value):
    piece_rows = lax.all_gather(normed, "tensor", axis=0, tiled=True)
    row_count = piece_rows.shape[0]
    request_count = piece_rows.shape[1]
    positions = (prefix_here[None, :] + jnp.arange(row_count, dtype=jnp.int32)[:, None]).astype(
        jnp.float32
    )
    queries = jnp.einsum("nsd,df->nsf", piece_rows, w_query, preferred_element_type=jnp.float32)
    queries = rotate(queries.reshape(row_count, request_count, -1, HD), positions)
    keys_new = jnp.einsum("nsd,df->nsf", piece_rows, w_key, preferred_element_type=jnp.float32)
    keys_new = rotate(keys_new.reshape(row_count, request_count, -1, HD), positions)
    values_new = jnp.einsum("nsd,df->nsf", piece_rows, w_value, preferred_element_type=jnp.float32)
    return jnp.concatenate(
        [
            queries.reshape(row_count, request_count, -1).astype(jnp.bfloat16),
            keys_new.reshape(row_count, request_count, -1).astype(jnp.bfloat16),
            values_new.astype(jnp.bfloat16),
        ],
        axis=-1,
    )


def attend_slots(packed, cache_keys, cache_values, slot_prefix, slot_length, q_width, kv_width):
    span_rows = packed.shape[0]
    slot_count = packed.shape[1]
    kv_heads = kv_width // HD
    groups = q_width // kv_width
    prefix = cache_keys.shape[1]
    score_scale = HD ** (-0.5)
    queries = packed[..., :q_width].reshape(span_rows, slot_count, kv_heads, groups, HD)
    keys_new = packed[..., q_width : q_width + kv_width].reshape(
        span_rows, slot_count, kv_heads, HD
    )
    values_new = packed[..., q_width + kv_width :].reshape(span_rows, slot_count, kv_heads, HD)
    keys_old = cache_keys.reshape(slot_count, prefix, kv_heads, HD)
    values_old = cache_values.reshape(slot_count, prefix, kv_heads, HD)
    score_old = (
        jnp.einsum("csgmd,spgd->sgmcp", queries, keys_old, preferred_element_type=jnp.float32)
        * score_scale
    )
    score_new = (
        jnp.einsum("csgmd,jsgd->sgmcj", queries, keys_new, preferred_element_type=jnp.float32)
        * score_scale
    )
    keep_old = jnp.arange(prefix, dtype=jnp.int32)[None, :] < slot_prefix[:, None]
    row_index = jnp.arange(span_rows, dtype=jnp.int32)
    keep_new = (row_index[None, None, :] < slot_length[:, None, None]) & (
        row_index[None, None, :] <= row_index[None, :, None]
    )
    score_old = jnp.where(keep_old[:, None, None, None, :], score_old, masked)
    score_new = jnp.where(keep_new[:, None, None, :, :], score_new, masked)
    exp_old = jnp.exp(score_old)
    exp_new = jnp.exp(score_new)
    denominator = jnp.sum(exp_old, axis=-1, keepdims=True) + jnp.sum(
        exp_new, axis=-1, keepdims=True
    )
    weight_old = (exp_old / denominator).astype(jnp.bfloat16)
    weight_new = (exp_new / denominator).astype(jnp.bfloat16)
    mixed = jnp.einsum(
        "sgmcp,spgd->csgmd", weight_old, values_old, preferred_element_type=jnp.float32
    )
    mixed = mixed + jnp.einsum(
        "sgmcj,jsgd->csgmd", weight_new, values_new, preferred_element_type=jnp.float32
    )
    return mixed.astype(jnp.bfloat16).reshape(span_rows, slot_count, q_width)


def local(
    hidden_rows,
    norm_gain,
    w_query,
    w_key,
    w_value,
    w_out,
    cache_keys,
    cache_values,
    slot_of_request,
    span_length,
    prefix_length,
):
    data_size = lax.axis_size("dp")
    data_index = lax.axis_index("dp")
    per_device = hidden_rows.shape[1]
    q_width = w_query.shape[1]
    kv_width = w_key.shape[1]
    all_requests = slot_of_request.shape[0]
    request_ids = jnp.arange(all_requests, dtype=jnp.int32)
    devices = jnp.arange(data_size, dtype=jnp.int32)
    first_request = data_index * per_device
    my_slots = lax.dynamic_slice_in_dim(slot_of_request, first_request, per_device)
    send_table = (devices[:, None] == my_slots[None, :] // per_device).astype(jnp.bfloat16)
    slot_match = (
        slot_of_request[None, :]
        == (first_request + jnp.arange(per_device, dtype=jnp.int32))[:, None]
    )
    source_match = request_ids[None, :] // per_device == devices[:, None]
    recv_table = jnp.any(slot_match[:, None, :] & source_match[None, :, :], axis=-1).astype(
        jnp.bfloat16
    )
    slot_prefix = jnp.sum(jnp.where(slot_match, prefix_length[None, :], 0), axis=1)
    slot_length = jnp.sum(jnp.where(slot_match, span_length[None, :], 0), axis=1)
    normed = normalize(hidden_rows, norm_gain)
    outgoing = jnp.einsum(
        "js,csf->jcf", send_table, normed, preferred_element_type=jnp.float32
    ).astype(jnp.bfloat16)
    incoming = lax.all_to_all(outgoing, "dp", split_axis=0, concat_axis=0, tiled=True)
    slot_rows = jnp.einsum(
        "sj,jcf->csf", recv_table, incoming, preferred_element_type=jnp.float32
    ).astype(jnp.bfloat16)
    packed = project_group(slot_rows, slot_prefix, w_query, w_key, w_value)
    mixed = attend_slots(
        packed, cache_keys, cache_values, slot_prefix, slot_length, q_width, kv_width
    )
    outgoing_back = jnp.einsum(
        "sj,csf->jcf", recv_table, mixed, preferred_element_type=jnp.float32
    ).astype(jnp.bfloat16)
    returned = lax.all_to_all(outgoing_back, "dp", split_axis=0, concat_axis=0, tiled=True)
    request_heads = jnp.einsum(
        "js,jcf->csf", send_table, returned, preferred_element_type=jnp.float32
    ).astype(jnp.bfloat16)
    span_rows = request_heads.shape[0]
    flat_heads = request_heads.reshape(span_rows * per_device, q_width)
    summed = lax.psum_scatter(
        jnp.dot(flat_heads, w_out, preferred_element_type=jnp.float32).astype(jnp.bfloat16),
        "tensor",
        scatter_dimension=0,
        tiled=True,
    ).astype(jnp.float32)
    return summed.reshape(hidden_rows.shape[0], per_device, -1).astype(jnp.bfloat16)


def solution(mesh):
    placed = (
        P("tensor", "dp", None),
        P(),
        P(None, "tensor"),
        P(None, "tensor"),
        P(None, "tensor"),
        P("tensor", None),
        P("dp", None, "tensor"),
        P("dp", None, "tensor"),
        P(),
        P(),
        P(),
    )
    return jax.shard_map(
        local, mesh=mesh, in_specs=placed, out_specs=P("tensor", "dp", None), check_vma=False
    )
```

profile of v0, /device:TPU:1, one launch (start us, length us, event | category | flops | bytes accessed | tf_op | source)
XLA Modules:
  0.0 441.8 jit_solution(15629852325169047121)
XLA Ops:
  6.5 0.0 copy-start
  6.5 2.6 fusion.16
  9.1 0.7 and_select_fusion
  9.8 7.6 %convolution_convert_fusion.1 = bf16[16,32,8192]{2,0,1:T(8,128)(2,1)} fusion(bf16[32,2,8192]{2,1,0:T(2,128)(2,1)} %param.11, f32[8192]{0:T(1024)} %param.12, f32[32,2]{1,0:T(8,128)S(1)} %add_rsqrt_fusion, s32[2]{0:T(128)S(1)} %and_select_fusion), kind=kOutput, calls=%fused_computation.6 | convolution fusion | flops 23068704 | bytes 9470216 | tf_op jit(solution)/shard_map/js,csf->jcf/dot_general | solution.py:138
  17.4 11.2 %copy.63 = bf16[16,32,8192]{2,1,0:T(8,128)(2,1)} copy(bf16[16,32,8192]{2,0,1:T(8,128)(2,1)} %convolution_convert_fusion.1) | data formatting | bytes 16777216 | tf_op jit(solution)/shard_map/convert_element_type | solution.py:140
  28.6 0.0 copy-start.4
  28.6 0.0 copy-start.5
  28.6 0.0 copy-start.6
  28.7 7.8 %all-to-all-start = ((bf16[16,32,8192]{2,1,0:T(8,128)(2,1)}), bf16[16,32,8192]{2,1,0:T(8,128)(2,1)}, u32[]{:S(2)}, u32[]{:S(2)}) async-start(bf16[16,32,8192]{2,1,0:T(8,128)(2,1)} %copy.63), calls=%async_computation | async-start | bytes 16777216 | tf_op jit(solution)/shard_map/all_to_all | solution.py:141
  36.4 0.5 all-gather.2.cloned.1.call-start
  37.0 0.0 copy-done.4
  37.0 0.0 copy-done.5
  37.0 0.0 copy-done.6
  37.0 0.2 select_reduce_fusion
  37.2 0.1 and_reduce_fusion
  37.3 145.3 %all-to-all-done = bf16[16,32,8192]{2,1,0:T(8,128)(2,1)} async-done(((bf16[16,32,8192]{2,1,0:T(8,128)(2,1)}), bf16[16,32,8192]{2,1,0:T(8,128)(2,1)}, u32[]{:S(2)}, u32[]{:S(2)}) %all-to-all-start) | async-done | bytes 8388640 | tf_op jit(solution)/shard_map/all_to_all | solution.py:141
  182.6 9.4 %fusion.3 = bf16[32,2,8192]{2,1,0:T(2,128)(2,1)} fusion(bf16[16,32,8192]{2,1,0:T(8,128)(2,1)} %all-to-all-done, pred[2,16]{1,0:T(4,128)(4,1)S(1)} %and_reduce_fusion), kind=kOutput, calls=%fused_computation.8 | convolution fusion | flops 17301504 | bytes 9437216 | tf_op jit(solution)/shard_map/sj,jcf->csf/dot_general | solution.py:142
  192.0 0.0 all-gather.2.cloned.1.call-update
  192.0 0.2 reduce-scatter.2.cloned.1.call-start
  192.3 0.1 iota_compare_fusion.3
  192.4 0.1 add_convert_fusion.1
  192.4 0.1 broadcast_and_fusion
  192.6 1.7 multiply_cosine_fusion
  194.3 0.1 iota_compare_fusion.1
  194.4 53.7 %all-gather.2.cloned.1.call-done = bf16[256,2,8192]{2,1,0:T(2,128)(2,1)} async-done(((bf16[32,2,8192]{2,1,0:T(2,128)(2,1)}), bf16[256,2,8192]{2,1,0:T(2,128)(2,1)}) %all-gather.2.cloned.1.call-update) | async-done | bytes 8388624 | tf_op jit(solution)/shard_map/all_gather | solution.py:37
  248.1 0.0 copy-start.7
  248.1 8.9 %fusion.38 = f32[256,2,1,128]{0,3,1,2:T(8,128)S(1)} fusion(bf16[8192,128]{1,0:T(8,128)(2,1)} %param.14, bf16[256,2,8192]{2,1,0:T(2,128)(2,1)} %all-gather.2.cloned.1.call-done), kind=kOutput, calls=%fused_computation.38 | convolution fusion | flops 1073741824 | bytes 10747904 | tf_op jit(solution)/shard_map/nsd,df->nsf/dot_general | solution.py:45
  256.9 1.2 fusion.78
  258.2 0.0 copy-done.7
  258.2 12.8 %fusion.6 = f32[256,2,512]{2,0,1:T(8,128)} fusion(bf16[8192,512]{1,0:T(8,128)(2,1)} %param.13, bf16[256,2,8192]{2,1,0:T(2,128)(2,1)S(1)} %copy-done.7), kind=kOutput, calls=%fused_computation.11 | convolution fusion | flops 4294967296 | bytes 17825792 | tf_op jit(solution)/shard_map/nsd,df->nsf/dot_general | solution.py:43
  271.0 1.6 reshape.282
  272.5 0.6 fusion.91
  273.1 1.2 subtract_convert_fusion
  274.4 0.0 copy-start.2
  274.4 0.0 copy-start.3
  274.4 9.1 %fusion.2 = (f32[2,4,256]{2,1,0:T(4,128)S(1)}, f32[2,256,4,2048]{3,1,2,0:T(8,128)}) fusion(pred[2,2048]{1,0:T(4,128)(4,1)S(1)} %iota_compare_fusion.1, bf16[2,2048,128]{2,1,0:T(8,128)(2,1)} %param.17, bf16[256,2,4,64]{3,0,2,1:T(8,128)(2,1)S(1)} %get-tuple-element.9, bf16[256,2,4,64]{3,0,2,1:T(8,128)(2,1)S(1)} %get-tuple-element.8), kind=kOutput, calls=%fused_computation.4 | convolution fusion | flops 1087371264 | bytes 18362368 | tf_op jit(solution)/shard_map/csgmd,spgd->sgmcp/dot_general | solution.py:73
  283.5 0.0 copy-done.2
  283.5 0.0 copy-done.3
  283.5 2.1 fusion.22
  285.6 0.0 copy-done
  285.6 0.0 copy-start.8
  285.6 14.5 %fusion.57 = f32[2,128,4,256]{3,1,2,0:T(8,128)} fusion(f32[2,256,256,4]{2,1,3,0:T(8,128)} %get-tuple-element.19, f32[2,4,256]{2,1,0:T(4,128)S(1)} %add.80, pred[2,256,256]{1,2,0:T(8,128)(4,1)S(1)} %broadcast_and_fusion, bf16[8192,128]{1,0:T(8,128)(2,1)S(1)} %copy-done, bf16[256,2,8192]{2,1,0:T(2,128)(2,1)} %all-gather.2.cloned.1.call-done), kind=kOutput, calls=%fused_computation.44 | convolution fusion | flops 1210122240 | bytes 13770752 | tf_op jit(solution)/shard_map/sgmcj,jsgd->csgmd/dot_general | solution.py:97
  300.1 0.0 copy-done.8
  300.1 8.1 %fusion.32 = bf16[2,128,4,256]{3,1,2,0:T(8,128)(2,1)S(1)} fusion(f32[2,128,4,256]{3,1,2,0:T(8,128)} %fusion.57, f32[2,4,256]{2,1,0:T(4,128)S(1)} %add.80, f32[2,256,4,2048]{3,1,2,0:T(8,128)} %get-tuple-element.17, pred[2,2048]{1,0:T(4,128)(4,1)S(1)} %iota_compare_fusion.1, bf16[2,2048,128]{2,1,0:T(8,128)(2,1)S(1)} %copy-done.8), kind=kOutput, calls=%fused_computation.36 | convolution fusion | flops 1091043328 | bytes 19410944 | tf_op jit(solution)/shard_map/sgmcp,spgd->csgmd/dot_general | solution.py:94
  308.2 0.5 copy.75
  308.8 1.6 convolution_convert_fusion.3
  310.4 2.4 copy.76
  312.8 56.0 %all_to_all.10 = bf16[16,256,512]{2,1,0:T(8,128)(2,1)S(1)} all-to-all(bf16[16,256,512]{2,1,0:T(8,128)(2,1)S(1)} %copy.76), channel_id=1, replica_groups=mesh['dp'=16,'tensor'=8] {'dp'}, dimensions={0} | all-to-all | bytes 8388608 | tf_op jit(solution)/shard_map/all_to_all | solution.py:152
  368.8 2.5 fusion.35
  371.3 0.2 reshape.287
  371.5 0.0 copy-start.1
  371.5 10.2 %convolution_convert_fusion = bf16[512,8192]{1,0:T(8,128)(2,1)} fusion(bf16[512,512]{1,0:T(8,128)(2,1)S(1)} %reshape.287, bf16[512,8192]{1,0:T(8,128)(2,1)} %param.16), kind=kOutput, calls=%fused_computation.5 | convolution fusion | flops 4299161600 | bytes 17301504 | tf_op jit(solution)/shard_map/dot_general | solution.py:159
  381.7 0.0 reduce-scatter.2.cloned.1.call-update
  381.8 50.2 %reduce-scatter.2.cloned.1.call-done = bf16[64,8192]{1,0:T(8,128)(2,1)} async-done(((bf16[512,8192]{1,0:T(8,128)(2,1)}), bf16[64,8192]{1,0:T(8,128)(2,1)}) %reduce-scatter.2.cloned.1.call-update) | async-done | bytes 1048592 | tf_op jit(solution)/shard_map/reduce_scatter | solution.py:158
  432.0 2.5 convert_element_type.82
  434.5 0.0 copy-done.1
  (7 shorter events, 0.1 us)
Async XLA Ops:
  6.5 279.1 %copy-start = (bf16[8192,128]{1,0:T(8,128)(2,1)S(1)}, bf16[8192,128]{1,0:T(8,128)(2,1)}, u32[]{:S(2)}) copy-start(bf16[8192,128]{1,0:T(8,128)(2,1)} %param.15) | copy-start | bytes 6291460
  28.6 8.3 %copy-start.4 = (s32[32]{0:T(128)S(1)}, s32[32]{0:T(128)}, u32[]{:S(2)}) copy-start(s32[32]{0:T(128)} %param.19) | copy-start | bytes 388
  28.6 8.3 %copy-start.5 = (s32[32]{0:T(128)S(1)}, s32[32]{0:T(128)}, u32[]{:S(2)}) copy-start(s32[32]{0:T(128)} %param.20) | copy-start | bytes 388
  28.6 8.4 %copy-start.6 = (s32[32]{0:T(128)S(1)}, s32[32]{0:T(128)}, u32[]{:S(2)}) copy-start(s32[32]{0:T(128)} %param.21) | copy-start | bytes 388
  28.7 153.9 %all-to-all-start = ((bf16[16,32,8192]{2,1,0:T(8,128)(2,1)}), bf16[16,32,8192]{2,1,0:T(8,128)(2,1)}, u32[]{:S(2)}, u32[]{:S(2)}) async-start(bf16[16,32,8192]{2,1,0:T(8,128)(2,1)} %copy.63), calls=%async_computation | async-start | bytes 16777216 | tf_op jit(solution)/shard_map/all_to_all | solution.py:141
  36.4 211.6 %all-gather.2.cloned.1.call-start = ((), (), s32[]{:S(2)}) async-start(), calls=%async_computation.3 | async-start | bytes 9437184 | tf_op jit(solution)/shard_map/all_gather | solution.py:37
  192.0 240.0 %reduce-scatter.2.cloned.1.call-start = ((), (), s32[]{:S(2)}) async-start(), calls=%async_computation.4 | async-start | bytes 9437184 | tf_op jit(solution)/shard_map/reduce_scatter | solution.py:158
  248.1 10.1 %copy-start.7 = (bf16[256,2,8192]{2,1,0:T(2,128)(2,1)S(1)}, bf16[256,2,8192]{2,1,0:T(2,128)(2,1)}, u32[]{:S(2)}) copy-start(bf16[256,2,8192]{2,1,0:T(2,128)(2,1)} %all-gather.2.cloned.1.call-done) | copy-start | bytes 25165828
  274.4 9.1 %copy-start.2 = (bf16[256,2,64]{0,2,1:T(8,128)(2,1)S(1)}, bf16[256,2,64]{0,2,1:T(8,128)(2,1)}, u32[]{:S(2)}) copy-start(bf16[256,2,64]{0,2,1:T(8,128)(2,1)} %get-tuple-element.12) | copy-start | bytes 196612
  274.4 9.1 %copy-start.3 = (bf16[256,2,64]{0,2,1:T(8,128)(2,1)S(1)}, bf16[256,2,64]{0,2,1:T(8,128)(2,1)}, u32[]{:S(2)}) copy-start(bf16[256,2,64]{0,2,1:T(8,128)(2,1)} %get-tuple-element.13) | copy-start | bytes 196612
  285.6 14.5 %copy-start.8 = (bf16[2,2048,128]{2,1,0:T(8,128)(2,1)S(1)}, bf16[2,2048,128]{2,1,0:T(8,128)(2,1)}, u32[]{:S(2)}) copy-start(bf16[2,2048,128]{2,1,0:T(8,128)(2,1)} %param.18) | copy-start | bytes 3145732
  371.5 63.0 %copy-start.1 = (bf16[8192,128]{1,0:T(8,128)(2,1)S(1)}, bf16[8192,128]{1,0:T(8,128)(2,1)}, u32[]{:S(2)}) copy-start(bf16[8192,128]{1,0:T(8,128)(2,1)} %param.15) | copy-start | bytes 6291460
Sparse Core Ops, SparseCore 0:
  192.1 55.8 all-gather.1
  381.9 50.0 reduce-scatter.1
where the time goes:
time: 449 us; the launch traced here: 442 us
  waiting for transfers between devices  249 us (55%)
  matrix products  86.9 us (19%)
  blocking collectives  56 us (12%)
  local copies, waits for them, and re-layouts  19 us (4%)
  between operations  14 us (3%)
  starting transfers between devices  8.49 us (2%)
  other arithmetic  8.21 us (2%)
    all_to_all x1, waiting for transfers between devices, local(): lax.all_to_all(outgoing, 'dp', split_axis=0, concat_axis=0, tiled=True)  145 us
    all_to_all x1, blocking collectives, local(): lax.all_to_all(outgoing_back, 'dp', split_axis=0, concat_axis=0, tiled=True)  56 us
    all_gather x1, waiting for transfers between devices, project_group(): piece_rows = lax.all_gather(normed, 'tensor', axis=0, tiled=True)  53.7 us
    reduce_scatter x1, waiting for transfers between devices, local(): lax.psum_scatter(jnp.dot(flat_heads, w_out, preferred_element_type=jnp.fl...  50.2 us
    dot_general x1, matrix products, attend_slots(): jnp.einsum('sgmcj,jsgd->csgmd', weight_new, values_new, preferred_element...  14.5 us
    dot_general x1, matrix products, project_group(): jnp.einsum('nsd,df->nsf', piece_rows, w_query, preferred_element_type=jnp...  12.8 us
    convert_element_type x1, local copies, waits for them, and re-layouts, local(): outgoing = jnp.einsum('js,csf->jcf', send_table, normed, preferred_elemen...  11.2 us
    dot_general x1, matrix products, local(): jnp.dot(flat_heads, w_out, preferred_element_type=jnp.float32)  10.2 us
  transfers between devices with their start and end apart: 3, of which 3 were waited for; matrix products, arithmetic and copies ran while one was open for 1% of the time, Pallas kernels for 0%

commit v1 on v0

v1 whole, which is shorter than its diff:
```python
import functools

import jax
import jax.numpy as jnp
from jax import lax
from jax.experimental import pallas as pl
from jax.experimental.pallas import tpu as pltpu
from jax.sharding import PartitionSpec as P

HD = 128
rope_base = 500000.0
norm_eps = 1e-05
masked = -1e30
log2e = 1.4426950408889634
MESH = pl.DeviceIdType.MESH


def peers():
    n = lax.axis_size("tensor")
    t = lax.axis_index("tensor")
    core = lax.rem(t, 2)
    return t, core, lax.rem(t + 2, n), lax.rem(t + n - 2, n), t + 1 - 2 * core


def greet(devices):
    barrier = pltpu.get_barrier_semaphore()
    for device in devices:
        pl.semaphore_signal(barrier, inc=1, device_id={"tensor": device}, device_id_type=MESH)
    pl.semaphore_wait(barrier, len(devices))


def remote(source, target, send_sem, recv_sem, device):
    return pltpu.make_async_remote_copy(
        src_ref=source,
        dst_ref=target,
        send_sem=send_sem,
        recv_sem=recv_sem,
        device_id={"tensor": device},
        device_id_type=MESH,
    )


TO_RIGHT, TO_LEFT, TO_SIB, ON_RIGHT, ON_LEFT, SIB_LEFT, SIB_RIGHT, SIB_FAR0, SIB_FAR1 = range(9)


def gather_project_kernel(
    chunks, x_ref, wq_ref, wk_ref, wv_ref, cos_ref, sin_ref, out_ref,
    rows, weights, total, w_sem, x_sem, send_sem, recv_sem,
):
    t, core, right, left, sib = peers()
    n = lax.axis_size("tensor")
    block = x_ref.shape[1]
    width = rows.shape[-1]
    q_width, kv_width = wq_ref.shape[1], wk_ref.shape[1]
    far = lax.rem(t + n // 2, n)

    def at(device):
        return pl.ds(pl.multiple_of(device * block, block), block)

    def piece(k, device):
        return rows.at[k, :, at(device), :]

    def half(k, which, device):
        return rows.at[k, which, at(device), :]

    def message(kind, k, view, device):
        return remote(view, view, send_sem.at[kind, k], recv_sem.at[kind, k], device)

    x_copies = [
        pltpu.make_async_copy(
            x_ref.at[:, :, pl.ds(k * width, width)], piece(k, t), x_sem.at[k]
        )
        for k in range(chunks)
    ]
    for copy in x_copies:
        copy.start()
    w_copies = []
    for index, (ref, start, size) in enumerate(
        ((wq_ref, 0, q_width), (wk_ref, q_width, kv_width), (wv_ref, q_width + kv_width, kv_width))
    ):
        copy = pltpu.make_async_copy(ref, weights.at[:, pl.ds(start, size)], w_sem.at[index])
        w_copies.append(copy)
    greet((right, left, sib))
    for k in range(chunks):
        x_copies[k].wait()
        message(TO_RIGHT, k, piece(k, t), right).start()
        message(TO_LEFT, k, piece(k, t), left).start()
        message(TO_SIB, k, piece(k, t), sib).start()
    for copy in w_copies:
        copy.start()
    total[...] = jnp.zeros_like(total)

    def onward(k, carry):
        message(TO_RIGHT, k, piece(k, left), right).wait_recv()
        message(ON_RIGHT, k, half(k, 0, left), right).start()
        message(SIB_LEFT, k, piece(k, left), sib).start()
        message(TO_LEFT, k, piece(k, right), left).wait_recv()
        message(ON_LEFT, k, half(k, 1, right), left).start()
        message(SIB_RIGHT, k, piece(k, right), sib).start()
        return carry

    lax.fori_loop(0, chunks, onward, 0)
    for copy in w_copies:
        copy.wait()
    sib_left, sib_right, sib_far = (
        left + 1 - 2 * core, right + 1 - 2 * core, far + 1 - 2 * core
    )

    def multiply(k, carry):
        @pl.when(k < chunks)
        def _():
            message(ON_RIGHT, k, half(k, 0, far), right).wait_recv()
            message(SIB_FAR0, k, half(k, 0, far), sib).start()
            message(ON_LEFT, k, half(k, 1, far), left).wait_recv()
            message(SIB_FAR1, k, half(k, 1, far), sib).start()

        @pl.when(k > 0)
        def _():
            j = k - 1
            message(TO_SIB, j, piece(j, sib), sib).wait_recv()
            message(SIB_LEFT, j, piece(j, sib_left), sib).wait_recv()
            message(SIB_RIGHT, j, piece(j, sib_right), sib).wait_recv()
            message(SIB_FAR0, j, half(j, 0, sib_far), sib).wait_recv()
            message(SIB_FAR1, j, half(j, 1, sib_far), sib).wait_recv()
            depth = pl.ds(pl.multiple_of(j * width, width), width)
            for r in range(rows.shape[1]):
                total[r] += jnp.dot(
                    rows[j, r], weights[depth, :], preferred_element_type=jnp.float32
                )

        return carry

    lax.fori_loop(0, chunks + 1, multiply, 0)
    half_head = HD // 2
    for r in range(rows.shape[1]):
        cosine, sine = cos_ref[r], sin_ref[r]
        for h in range((q_width + kv_width) // HD):
            columns = pl.ds(h * HD, HD)
            value = total[r, :, columns]
            value = value * cosine + pltpu.roll(value, half_head, axis=1) * sine
            if h < q_width // HD:
                value = value * (HD ** (-0.5) * log2e)
            out_ref[r, :, columns] = value.astype(out_ref.dtype)
        columns = pl.ds(q_width + kv_width, kv_width)
        out_ref[r, :, columns] = total[r, :, columns].astype(out_ref.dtype)

    def drain(k, carry):
        for kind in range(3):
            message(kind, k, piece(k, t), (right, left, sib)[kind]).wait_send()
        message(ON_RIGHT, k, half(k, 0, left), right).wait_send()
        message(ON_LEFT, k, half(k, 1, right), left).wait_send()
        message(SIB_LEFT, k, piece(k, left), sib).wait_send()
        message(SIB_RIGHT, k, piece(k, right), sib).wait_send()
        message(SIB_FAR0, k, half(k, 0, far), sib).wait_send()
        message(SIB_FAR1, k, half(k, 1, far), sib).wait_send()
        return carry

    lax.fori_loop(0, chunks, drain, 0)


def gather_project(x, wq, wk, wv, cosine, sine, chunks=8):
    requests, block, depth = x.shape
    n = lax.axis_size("tensor")
    width = wq.shape[1] + wk.shape[1] + wv.shape[1]
    any_space = pl.BlockSpec(memory_space=pl.ANY)
    vmem = pl.BlockSpec(memory_space=pltpu.VMEM)
    return pl.pallas_call(
        functools.partial(gather_project_kernel, chunks),
        out_shape=jax.ShapeDtypeStruct((requests, block * n, width), jnp.bfloat16),
        in_specs=[any_space] * 4 + [vmem] * 2,
        out_specs=vmem,
        scratch_shapes=[
            pltpu.VMEM((chunks, requests, block * n, depth // chunks), jnp.bfloat16),
            pltpu.VMEM((depth, width), jnp.bfloat16),
            pltpu.VMEM((requests, block * n, width), jnp.float32),
            pltpu.SemaphoreType.DMA((3,)),
            pltpu.SemaphoreType.DMA((chunks,)),
            pltpu.SemaphoreType.DMA((9, chunks)),
            pltpu.SemaphoreType.DMA((9, chunks)),
        ],
        compiler_params=pltpu.CompilerParams(
            collective_id=0, has_side_effects=True, vmem_limit_bytes=48 << 20
        ),
        name="gather_project",
    )(x, wq, wk, wv, cosine, sine)


def attend_kernel(order_ref, prefix_ref, span_ref, x_ref, k_ref, v_ref, out_ref):
    packet = pl.program_id(0)
    span_rows = x_ref.shape[1]
    prefix_rows = k_ref.shape[1]
    q_width = out_ref.shape[2]
    prefix, span = prefix_ref[packet], span_ref[packet]
    keys_new = x_ref[0, :, q_width : q_width + HD]
    values_new = x_ref[0, :, q_width + HD :]
    old_column = lax.broadcasted_iota(jnp.int32, (1, prefix_rows), 1)
    old_bias = jnp.where(old_column < prefix, 0.0, masked)
    row = lax.broadcasted_iota(jnp.int32, (span_rows, span_rows), 0)
    column = lax.broadcasted_iota(jnp.int32, (span_rows, span_rows), 1)
    new_bias = jnp.where((column <= row) & (column < span), 0.0, masked)
    contract = (((1,), (1,)), ((), ()))
    for h in range(q_width // HD):
        query = x_ref[0, :, h * HD : (h + 1) * HD]
        old = (
            lax.dot_general(query, k_ref[0], contract, preferred_element_type=jnp.float32)
            + old_bias
        )
        new = (
            lax.dot_general(query, keys_new, contract, preferred_element_type=jnp.float32)
            + new_bias
        )
        top = jnp.maximum(
            jnp.max(old, axis=1, keepdims=True), jnp.max(new, axis=1, keepdims=True)
        )
        old = jnp.exp2(old - top)
        new = jnp.exp2(new - top)
        weight_sum = jnp.sum(old, axis=1, keepdims=True) + jnp.sum(new, axis=1, keepdims=True)
        mixed = jnp.dot(old.astype(jnp.bfloat16), v_ref[0], preferred_element_type=jnp.float32)
        mixed += jnp.dot(
            new.astype(jnp.bfloat16), values_new, preferred_element_type=jnp.float32
        )
        out_ref[0, :, h * HD : (h + 1) * HD] = (mixed / weight_sum).astype(out_ref.dtype)


def attend(packets, cache_keys, cache_values, order, prefix, span, q_width):
    count, span_rows, width = packets.shape
    _, prefix_rows, kv_width = cache_keys.shape
    cache = pl.BlockSpec((1, prefix_rows, kv_width), lambda i, order, p, s: (order[i], 0, 0))
    return pl.pallas_call(
        attend_kernel,
        out_shape=jax.ShapeDtypeStruct((count, span_rows, q_width), jnp.bfloat16),
        grid_spec=pltpu.PrefetchScalarGridSpec(
            num_scalar_prefetch=3,
            grid=(count,),
            in_specs=[
                pl.BlockSpec((1, span_rows, width), lambda i, *_: (i, 0, 0)),
                cache,
                cache,
            ],
            out_specs=pl.BlockSpec((1, span_rows, q_width), lambda i, *_: (i, 0, 0)),
        ),
        compiler_params=pltpu.CompilerParams(vmem_limit_bytes=48 << 20),
        name="attend",
    )(order, prefix, span, packets, cache_keys, cache_values)


SWAP, FAR_RIGHT, FAR_LEFT, SUM_RIGHT, SUM_LEFT = range(5)


def project_reduce_kernel(
    chunks, heads_ref, w_ref, out_ref,
    weights, mine, swap_out, swap_in, far_out, far_in, sum_out, sum_in, w_sem, send_sem, recv_sem,
):
    t, core, right, left, sib = peers()
    requests, block, _ = out_ref.shape
    chips = lax.axis_size("tensor") // 2
    width = swap_out.shape[-1]
    z = t // 2
    z_right, z_left, z_far = right // 2, left // 2, lax.rem(z + chips // 2, chips)

    def message(kind, j, source, target, device):
        return remote(source, target, send_sem.at[kind, j], recv_sem.at[kind, j], device)

    def swap(j):
        return message(SWAP, j, swap_out.at[j], swap_in.at[j], sib)

    def far_right(j):
        return message(FAR_RIGHT, j, far_out.at[j, 0], far_in.at[j, 0], right)

    def far_left(j):
        return message(FAR_LEFT, j, far_out.at[j, 1], far_in.at[j, 1], left)

    def sum_right(j):
        return message(SUM_RIGHT, j, sum_out.at[j, 0], sum_in.at[j, 0], right)

    def sum_left(j):
        return message(SUM_LEFT, j, sum_out.at[j, 1], sum_in.at[j, 1], left)

    w_copies = [
        pltpu.make_async_copy(
            w_ref.at[:, pl.ds(j * width, width)], weights.at[j], w_sem.at[j]
        )
        for j in range(chunks)
    ]
    for copy in w_copies:
        copy.start()
    greet((right, left, sib))

    def columns(j):
        return pl.ds(pl.multiple_of(j * width, width), width)

    def step(j, carry):
        @pl.when(j < chunks)
        def _():
            pltpu.make_async_copy(w_ref.at[:, columns(j)], weights.at[j], w_sem.at[j]).wait()
            for r in range(requests):
                part = jnp.dot(
                    heads_ref[r], weights[j], preferred_element_type=jnp.float32
                ).reshape(chips, 2, block, width)
                keep = jnp.where(core == 0, part[:, 0], part[:, 1])
                give = jnp.where(core == 0, part[:, 1], part[:, 0])
                mine[j, r] = keep
                swap_out[j, r] = give.astype(jnp.bfloat16)
            swap(j).start()

        @pl.when((j > 0) & (j <= chunks))
        def _():
            i = j - 1
            swap(i).wait_recv()
            for r in range(requests):
                mine[i, r] = mine[i, r] + swap_in[i, r].astype(jnp.float32)
            far_out[i, 0] = mine[i, 0, z_far].astype(jnp.bfloat16)
            far_out[i, 1] = mine[i, 1, z_far].astype(jnp.bfloat16)
            far_right(i).start()
            far_left(i).start()

        @pl.when(j > 1)
        def _():
            i = j - 2
            sum_out[i, 0, 1] = mine[i, 1, z_right].astype(jnp.bfloat16)
            sum_out[i, 1, 0] = mine[i, 0, z_left].astype(jnp.bfloat16)
            far_right(i).wait_recv()
            sum_out[i, 0, 0] = (
                mine[i, 0, z_right] + far_in[i, 0].astype(jnp.float32)
            ).astype(jnp.bfloat16)
            sum_right(i).start()
            far_left(i).wait_recv()
            sum_out[i, 1, 1] = (
                mine[i, 1, z_left] + far_in[i, 1].astype(jnp.float32)
            ).astype(jnp.bfloat16)
            sum_left(i).start()

        return carry

    lax.fori_loop(0, chunks + 2, step, 0)

    def finish(j, carry):
        sum_right(j).wait_recv()
        sum_left(j).wait_recv()
        for r in range(requests):
            out_ref[r, :, columns(j)] = (
                mine[j, r, z]
                + sum_in[j, 0, r].astype(jnp.float32)
                + sum_in[j, 1, r].astype(jnp.float32)
            ).astype(jnp.bfloat16)
        return carry

    lax.fori_loop(0, chunks, finish, 0)

    def drain(j, carry):
        swap(j).wait_send()
        far_right(j).wait_send()
        far_left(j).wait_send()
        sum_right(j).wait_send()
        sum_left(j).wait_send()
        return carry

    lax.fori_loop(0, chunks, drain, 0)


def project_reduce(heads, w_out, chunks=8):
    requests, span_rows, depth = heads.shape
    n = lax.axis_size("tensor")
    block = span_rows // n
    features = w_out.shape[1]
    width = features // chunks
    bf16, f32 = jnp.bfloat16, jnp.float32
    return pl.pallas_call(
        functools.partial(project_reduce_kernel, chunks),
        out_shape=jax.ShapeDtypeStruct((requests, block, features), bf16),
        in_specs=[pl.BlockSpec(memory_space=pltpu.VMEM), pl.BlockSpec(memory_space=pl.ANY)],
        out_specs=pl.BlockSpec(memory_space=pltpu.VMEM),
        scratch_shapes=[
            pltpu.VMEM((chunks, depth, width), bf16),
            pltpu.VMEM((chunks, requests, n // 2, block, width), f32),
            pltpu.VMEM((chunks, requests, n // 2, block, width), bf16),
            pltpu.VMEM((chunks, requests, n // 2, block, width), bf16),
            pltpu.VMEM((chunks, 2, block, width), bf16),
            pltpu.VMEM((chunks, 2, block, width), bf16),
            pltpu.VMEM((chunks, 2, requests, block, width), bf16),
            pltpu.VMEM((chunks, 2, requests, block, width), bf16),
            pltpu.SemaphoreType.DMA((chunks,)),
            pltpu.SemaphoreType.DMA((5, chunks)),
            pltpu.SemaphoreType.DMA((5, chunks)),
        ],
        compiler_params=pltpu.CompilerParams(
            collective_id=1, has_side_effects=True, vmem_limit_bytes=52 << 20
        ),
        name="project_reduce",
    )(heads, w_out)


def exchange(first, second, mask):
    size = lax.axis_size("dp")

    def swap(value, other):
        if other == 0:
            return value
        return lax.ppermute(value, "dp", [(i, i ^ other) for i in range(size)])

    def branch(other):
        return lambda a, b: (swap(a, 1), swap(b, other))

    return lax.switch(mask, [branch(other) for other in range(size)], first, second)


def local(
    hidden_rows, norm_gain, w_query, w_key, w_value, w_out, cache_keys, cache_values,
    slot_of_request, span_length, prefix_length,
):
    per_device = hidden_rows.shape[1]
    q_width = w_query.shape[1]
    data_index = lax.axis_index("dp")
    tensor_size = lax.axis_size("tensor")
    mine = lax.dynamic_slice_in_dim(slot_of_request, data_index * per_device, per_device)
    masks = jnp.bitwise_xor(mine // per_device, data_index)
    near = jnp.where(masks[0] == 1, 0, 1)
    mask = jnp.where(masks[0] == 1, masks[1], masks[0])

    floats = hidden_rows.astype(jnp.float32)
    normed = (
        floats * lax.rsqrt(jnp.mean(floats * floats, axis=-1, keepdims=True) + norm_eps) * norm_gain
    ).astype(jnp.bfloat16)
    normed = jnp.transpose(normed, (1, 0, 2))

    span_rows = hidden_rows.shape[0] * tensor_size
    prefix_here = lax.dynamic_slice_in_dim(prefix_length, data_index * per_device, per_device)
    frequency = rope_base ** (-(jnp.arange(HD // 2, dtype=jnp.float32) * 2.0 / HD))
    positions = (prefix_here[:, None] + jnp.arange(span_rows, dtype=jnp.int32)[None, :]).astype(
        jnp.float32
    )
    angles = positions[:, :, None] * frequency
    cosine, sine = jnp.cos(angles), jnp.sin(angles)
    cosine = jnp.concatenate([cosine, cosine], axis=-1)
    sine = jnp.concatenate([-sine, sine], axis=-1)
    packed = gather_project(normed, w_query, w_key, w_value, cosine, sine)

    flip = near == 1
    near_packet = jnp.where(flip, packed[1], packed[0])
    other_packet = jnp.where(flip, packed[0], packed[1])
    near_in, other_in = exchange(near_packet, other_packet, mask)

    slots = data_index * per_device + jnp.arange(per_device, dtype=jnp.int32)
    match = slot_of_request[None, :] == slots[:, None]
    request_of = jnp.sum(
        jnp.where(match, jnp.arange(slot_of_request.shape[0], dtype=jnp.int32)[None, :], 0), axis=1
    )
    slot_prefix = jnp.sum(jnp.where(match, prefix_length[None, :], 0), axis=1)
    slot_span = jnp.sum(jnp.where(match, span_length[None, :], 0), axis=1)
    from_near = jnp.bitwise_xor(request_of // per_device, data_index) == 1
    near_slot = jnp.where(from_near[0], 0, 1).astype(jnp.int32)
    order = jnp.stack([near_slot, 1 - near_slot])
    swapped = near_slot == 1
    prefix = jnp.where(swapped, slot_prefix[::-1], slot_prefix)
    span = jnp.where(swapped, slot_span[::-1], slot_span)
    mixed = attend(
        jnp.stack([near_in, other_in]), cache_keys, cache_values, order, prefix, span, q_width
    )
    near_back, other_back = exchange(mixed[0], mixed[1], mask)
    heads = jnp.stack(
        [jnp.where(flip, other_back, near_back), jnp.where(flip, near_back, other_back)]
    )
    result = project_reduce(heads, w_out)
    return jnp.transpose(result, (1, 0, 2))


def solution(mesh):
    placed = (
        P("tensor", "dp", None),
        P(),
        P(None, "tensor"),
        P(None, "tensor"),
        P(None, "tensor"),
        P("tensor", None),
        P("dp", None, "tensor"),
        P("dp", None, "tensor"),
        P(),
        P(),
        P(),
    )
    return jax.shard_map(
        local, mesh=mesh, in_specs=placed, out_specs=P("tensor", "dp", None), check_vma=False
    )
```

time: 449 us -> 132 us (0.29); the launches traced: 442 us -> 132 us
  waiting for transfers between devices: 249 us -> 15.9 us
  Pallas kernels: 0 us -> 97 us
  matrix products: 86.9 us -> 0 us
  blocking collectives: 56 us -> 0 us
  local copies, waits for them, and re-layouts: 19 us -> 3.9 us
  between operations: 14 us -> 2.23 us
    all_to_all x1 -> x0, waiting for transfers between devices: 145 us -> none  [local(): lax.all_to_all(outgoing, 'dp', split_axis=0, concat_axis=0, tiled=True)]
    pallas_call x0 -> x3, Pallas kernels: none -> 97 us  [the longest x1 44.6 us: gather_project(): pl.pallas_call(functools.partial(gather_project_kernel, chunks), out_shap...]
    dot_general x11 -> x0, matrix products: 86.9 us -> none  [the longest x1 14.5 us: attend_slots(): jnp.einsum('sgmcj,jsgd->csgmd', weight_new, values_new, preferred_element...]
    all_to_all x1 -> x0, blocking collectives: 56 us -> none  [local(): lax.all_to_all(outgoing_back, 'dp', split_axis=0, concat_axis=0, tiled=True)]
    all_gather x1 -> x0, waiting for transfers between devices: 53.7 us -> none  [project_group(): piece_rows = lax.all_gather(normed, 'tensor', axis=0, tiled=True)]
    reduce_scatter x1 -> x0, waiting for transfers between devices: 50.2 us -> none  [local(): lax.psum_scatter(jnp.dot(flat_heads, w_out, preferred_element_type=jnp.fl...]
    convert_element_type x3 -> x0, local copies, waits for them, and re-layouts: 16.1 us -> none  [the longest x1 11.2 us: local(): outgoing = jnp.einsum('js,csf->jcf', send_table, normed, preferred_elemen...]
    ppermute x0 -> x4, waiting for transfers between devices: none -> 15.9 us  [swap(): return lax.ppermute(value, 'dp', [(i, i ^ other) for i in range(size)])]
  transfers between devices with their start and end apart: 3 -> 4, of which waited for: 3 -> 4; matrix products, arithmetic and copies ran while one was open for 1% -> 0% of each run, Pallas kernels for 0% -> 0%
where the time goes in v1:
time: 132 us
  Pallas kernels  97 us (73%)
  waiting for transfers between devices  15.9 us (12%)
  starting transfers between devices  7.11 us (5%)
  other arithmetic  5.87 us (4%)
  local copies, waits for them, and re-layouts  3.9 us (3%)
  between operations  2.23 us (2%)
    pallas_call x1, Pallas kernels, gather_project(): pl.pallas_call(functools.partial(gather_project_kernel, chunks), out_shap...  44.6 us
    pallas_call x1, Pallas kernels, project_reduce(): pl.pallas_call(functools.partial(project_reduce_kernel, chunks), out_shap...  44 us
    ppermute x4, waiting for transfers between devices, swap(): return lax.ppermute(value, 'dp', [(i, i ^ other) for i in range(size)])  15.9 us
    pallas_call x1, Pallas kernels, attend(): pl.pallas_call(attend_kernel, out_shape=jax.ShapeDtypeStruct((count, span...  8.39 us
    ppermute x4, starting transfers between devices, swap(): return lax.ppermute(value, 'dp', [(i, i ^ other) for i in range(size)])  7.11 us
  transfers between devices with their start and end apart: 4, of which 4 were waited for; matrix products, arithmetic and copies ran while one was open for 0% of the time, Pallas kernels for 0%

profile of v1, /device:TPU:1, one launch (start us, length us, event | category | flops | bytes accessed | tf_op | source)
XLA Modules:
  0.0 132.1 jit_solution(11231484666732568611)
XLA Ops:
  0.0 0.0 copy-start.4
  0.0 0.0 copy-start.5
  0.0 0.8 dynamic_slice.7
  0.8 0.1 add_convert_fusion
  0.9 1.0 fusion.4
  1.9 0.0 copy-start
  1.9 0.0 copy-start.1
  1.9 0.2 pad_maximum_fusion.2
  2.1 0.0 copy-done.4
  2.2 1.2 fusion
  3.3 0.0 copy-done.5
  3.3 0.6 fusion.3.x_ref
  4.0 0.0 copy-done
  4.0 0.2 copy-done.1
  4.1 0.0 copy-start.6
  4.1 44.6 %gather_project.1 = bf16[2,256,768]{2,1,0:T(8,128)(2,1)S(1)} custom-call(bf16[2,32,8192]{2,1,0:T(8,128)(2,1)S(1)} %fusion.3.x_ref, bf16[8192,512]{1,0:T(8,128)(2,1)} %wq_ref.1, bf16[8192,128]{1,0:T(8,128)(2,1)S(1)} %copy-done, bf16[8192,128]{1,0:T(8,128)(2,1)S(1)} %copy-done.1, f32[2,256,128]{2,1,0:T(8,128)S(1)} %get-tuple-element.429.cos_ref, ...), custom_call_target="tpu_custom_call" | custom-call | tf_op jit(solution)/shard_map/gather_project/pallas_call | solution.py:167
  48.8 0.0 copy-done.6
  48.8 0.1 fusion.8
  48.9 0.6 fusion.9
  51.5 0.0 copy-start.7
  51.5 0.0 copy-start.8
  51.5 0.0 copy-start.3
  51.5 13.9 %conditional.2 = (bf16[1,256,768]{2,1,0:T(8,128)(2,1)}, bf16[1,256,768]{2,1,0:T(8,128)(2,1)}) conditional(s32[]{:T(128)} %clamp.4, (pred[]{:T(512)}, bf16[2,256,768]{2,1,0:T(8,128)(2,1)S(1)}) %tuple.168, (pred[]{:T(512)}, bf16[2,256,768]{2,1,0:T(8,128)(2,1)S(1)}) %tuple.168, (pred[]{:T(512)}, ...), branch_computations={%region_4.5_spmd, %region_5.6_spmd, %region_6.7_spmd, %region_7.8_... | conditional | flops 393216 | bytes 4718689 | solution.py:404
  51.6 0.1 select_bitcast_fusion.13
  51.6 1.4 %collective-permute-start.44 = (bf16[256,768]{1,0:T(8,128)(2,1)S(1)}, bf16[256,768]{1,0:T(8,128)(2,1)}, u32[]{:S(2)}, u32[]{:S(2)}) collective-permute-start(bf16[256,768]{1,0:T(8,128)(2,1)S(1)} %get-tuple-element.401), channel_id=1, source_target_pairs={{0,8},{8,0},{16,24},{24,16},{32,40},{40,32},{48,56},{56,48},{64,72... | collective-permute-start | bytes 1179656 | tf_op jit(solution)/shard_map/cond/branch_7_fun/ppermute | solution.py:399
  53.0 2.8 %collective-permute-start.45 = (bf16[256,768]{1,0:T(8,128)(2,1)S(1)}, bf16[256,768]{1,0:T(8,128)(2,1)}, u32[]{:S(2)}, u32[]{:S(2)}) collective-permute-start(bf16[256,768]{1,0:T(8,128)(2,1)S(1)} %get-tuple-element.400), channel_id=1, source_target_pairs={{0,56},{8,48},{16,40},{24,32},{32,24},{40,16},{48,8},{56,0},{64,12... | collective-permute-start | bytes 1179656 | tf_op jit(solution)/shard_map/cond/branch_7_fun/ppermute | solution.py:399
  55.8 6.5 %collective-permute-done.44 = bf16[256,768]{1,0:T(8,128)(2,1)} collective-permute-done((bf16[256,768]{1,0:T(8,128)(2,1)S(1)}, bf16[256,768]{1,0:T(8,128)(2,1)}, u32[]{:S(2)}, u32[]{:S(2)}) %collective-permute-start.44) | collective-permute-done | bytes 393248 | tf_op jit(solution)/shard_map/cond/branch_7_fun/ppermute | solution.py:399
  62.4 3.1 %collective-permute-done.45 = bf16[256,768]{1,0:T(8,128)(2,1)} collective-permute-done((bf16[256,768]{1,0:T(8,128)(2,1)S(1)}, bf16[256,768]{1,0:T(8,128)(2,1)}, u32[]{:S(2)}, u32[]{:S(2)}) %collective-permute-start.45) | collective-permute-done | bytes 393248 | tf_op jit(solution)/shard_map/cond/branch_7_fun/ppermute | solution.py:399
  65.4 0.0 copy-start.2
  65.5 1.3 pad_maximum_fusion.x_ref
  66.7 0.0 copy-done.7
  66.8 0.0 copy-done.8
  66.8 0.2 fusion.7
  67.0 0.1 rev.6
  67.1 0.1 rev.7
  67.3 0.1 pad_add_fusion.order_ref
  67.3 0.0 copy-done.3
  67.3 0.0 copy-done.2
  67.3 8.4 %attend.1 = bf16[2,256,512]{2,1,0:T(8,128)(2,1)S(1)} custom-call(s32[2]{0:T(128)S(1)} %pad_add_fusion.order_ref, s32[2]{0:T(128)S(1)} %get-tuple-element.428.prefix_ref, s32[2]{0:T(128)S(1)} %get-tuple-element.427.span_ref, bf16[2,256,768]{2,1,0:T(8,128)(2,1)S(1)} %pad_maximum_fusion.x_ref, bf16[2,2048,128]{2,1,0:T(8,128)(2,1)S(1)} %copy-done.2, ...), custom_call_target="tpu_custom_call" | custom-call | tf_op jit(solution)/shard_map/attend/pallas_call | solution.py:229
  75.8 9.3 %conditional.3 = (bf16[256,512]{1,0:T(8,128)(2,1)}, bf16[256,512]{1,0:T(8,128)(2,1)S(1)}) conditional(s32[]{:T(128)} %clamp.4, (bf16[256,512]{1,0:T(8,128)(2,1)S(1)}, bf16[256,512]{1,0:T(8,128)(2,1)S(1)}) %tuple.169, (bf16[256,512]{1,0:T(8,128)(2,1)S(1)}, bf16[256,512]{1,0:T(8,128)(2,1)S(1)}) %tuple.169, ...), branch_computations={%region_20.21_spmd, %region_21.22_spmd, %region_22.23_spmd, %regio... | conditional | bytes 2621536 | solution.py:404
  75.8 2.9 %collective-permute-start.14 = (bf16[256,512]{1,0:T(8,128)(2,1)S(1)}, bf16[256,512]{1,0:T(8,128)(2,1)S(1)}, u32[]{:S(2)}, u32[]{:S(2)}) collective-permute-start(bf16[256,512]{1,0:T(8,128)(2,1)S(1)} %get-tuple-element.358), channel_id=1, source_target_pairs={{0,56},{8,48},{16,40},{24,32},{32,24},{40,16},{48,8},{56,0},{64,12... | collective-permute-start | bytes 786440 | tf_op jit(solution)/shard_map/cond/branch_7_fun/ppermute | solution.py:399
  78.7 0.0 collective-permute-start.13
  78.7 5.8 %collective-permute-done.14 = bf16[256,512]{1,0:T(8,128)(2,1)S(1)} collective-permute-done((bf16[256,512]{1,0:T(8,128)(2,1)S(1)}, bf16[256,512]{1,0:T(8,128)(2,1)S(1)}, u32[]{:S(2)}, u32[]{:S(2)}) %collective-permute-start.14) | collective-permute-done | bytes 262176 | tf_op jit(solution)/shard_map/cond/branch_7_fun/ppermute | solution.py:399
  84.5 0.5 collective-permute-done.13
  85.1 1.0 select_bitcast_fusion.32
  86.0 0.1 pad_maximum_fusion.1.heads_ref
  86.1 44.0 %project_reduce.1 = bf16[2,32,8192]{2,1,0:T(8,128)(2,1)S(1)} custom-call(bf16[2,256,512]{2,1,0:T(8,128)(2,1)S(1)} %pad_maximum_fusion.1.heads_ref, bf16[512,8192]{1,0:T(8,128)(2,1)} %w_ref.1), custom_call_target="tpu_custom_call" | custom-call | tf_op jit(solution)/shard_map/project_reduce/pallas_call | solution.py:368
  130.1 2.1 %copy.15 = bf16[32,2,8192]{2,1,0:T(2,128)(2,1)} copy(bf16[32,2,8192]{2,0,1:T(8,128)(2,1)S(1)} %bitcast.108) | data formatting | bytes 2097152 | tf_op jit(solution)/shard_map/transpose | solution.py:464
  (7 shorter events, 0.1 us)
Async XLA Ops:
  0.0 2.1 %copy-start.4 = (bf16[32,2,8192]{2,1,0:T(2,128)(2,1)S(1)}, bf16[32,2,8192]{2,1,0:T(2,128)(2,1)}, u32[]{:S(2)}) copy-start(bf16[32,2,8192]{2,1,0:T(2,128)(2,1)} %param.43) | copy-start | bytes 3145732
  0.0 3.3 %copy-start.5 = (f32[8192]{0:T(1024)S(1)}, f32[8192]{0:T(1024)}, u32[]{:S(2)}) copy-start(f32[8192]{0:T(1024)} %param.44) | copy-start | bytes 98308
  1.9 2.1 %copy-start = (bf16[8192,128]{1,0:T(8,128)(2,1)S(1)}, bf16[8192,128]{1,0:T(8,128)(2,1)}, u32[]{:S(2)}) copy-start(bf16[8192,128]{1,0:T(8,128)(2,1)} %wk_ref.1) | copy-start | bytes 6291460
  1.9 2.2 %copy-start.1 = (bf16[8192,128]{1,0:T(8,128)(2,1)S(1)}, bf16[8192,128]{1,0:T(8,128)(2,1)}, u32[]{:S(2)}) copy-start(bf16[8192,128]{1,0:T(8,128)(2,1)} %wv_ref.1) | copy-start | bytes 6291460
  4.1 44.7 %copy-start.6 = (s32[32]{0:T(128)S(1)}, s32[32]{0:T(128)}, u32[]{:S(2)}) copy-start(s32[32]{0:T(128)} %param.51) | copy-start | bytes 388
  51.5 15.3 %copy-start.7 = (s32[32]{0:T(128)S(1)}, s32[32]{0:T(128)}, u32[]{:S(2)}) copy-start(s32[32]{0:T(128)} %param.52) | copy-start | bytes 388
  51.5 15.3 %copy-start.8 = (s32[32]{0:T(128)S(1)}, s32[32]{0:T(128)}, u32[]{:S(2)}) copy-start(s32[32]{0:T(128)} %param.53) | copy-start | bytes 388
  51.5 15.8 %copy-start.3 = (bf16[2,2048,128]{2,1,0:T(8,128)(2,1)S(1)}, bf16[2,2048,128]{2,1,0:T(8,128)(2,1)}, u32[]{:S(2)}) copy-start(bf16[2,2048,128]{2,1,0:T(8,128)(2,1)} %v_ref.1) | copy-start | bytes 3145732
  51.6 10.7 %collective-permute-start.44 = (bf16[256,768]{1,0:T(8,128)(2,1)S(1)}, bf16[256,768]{1,0:T(8,128)(2,1)}, u32[]{:S(2)}, u32[]{:S(2)}) collective-permute-start(bf16[256,768]{1,0:T(8,128)(2,1)S(1)} %get-tuple-element.401), channel_id=1, source_target_pairs={{0,8},{8,0},{16,24},{24,16},{32,40},{40,32},{48,56},{56,48},{64,72... | collective-permute-start | bytes 1179656 | tf_op jit(solution)/shard_map/cond/branch_7_fun/ppermute | solution.py:399
  53.0 12.4 %collective-permute-start.45 = (bf16[256,768]{1,0:T(8,128)(2,1)S(1)}, bf16[256,768]{1,0:T(8,128)(2,1)}, u32[]{:S(2)}, u32[]{:S(2)}) collective-permute-start(bf16[256,768]{1,0:T(8,128)(2,1)S(1)} %get-tuple-element.400), channel_id=1, source_target_pairs={{0,56},{8,48},{16,40},{24,32},{32,24},{40,16},{48,8},{56,0},{64,12... | collective-permute-start | bytes 1179656 | tf_op jit(solution)/shard_map/cond/branch_7_fun/ppermute | solution.py:399
  65.4 1.9 %copy-start.2 = (bf16[2,2048,128]{2,1,0:T(8,128)(2,1)S(1)}, bf16[2,2048,128]{2,1,0:T(8,128)(2,1)}, u32[]{:S(2)}) copy-start(bf16[2,2048,128]{2,1,0:T(8,128)(2,1)} %k_ref.1) | copy-start | bytes 3145732
  75.8 8.7 %collective-permute-start.14 = (bf16[256,512]{1,0:T(8,128)(2,1)S(1)}, bf16[256,512]{1,0:T(8,128)(2,1)S(1)}, u32[]{:S(2)}, u32[]{:S(2)}) collective-permute-start(bf16[256,512]{1,0:T(8,128)(2,1)S(1)} %get-tuple-element.358), channel_id=1, source_target_pairs={{0,56},{8,48},{16,40},{24,32},{32,24},{40,16},{48,8},{56,0},{64,12... | collective-permute-start | bytes 786440 | tf_op jit(solution)/shard_map/cond/branch_7_fun/ppermute | solution.py:399
  78.7 6.3 %collective-permute-start.13 = (bf16[256,512]{1,0:T(8,128)(2,1)S(1)}, bf16[256,512]{1,0:T(8,128)(2,1)}, u32[]{:S(2)}, u32[]{:S(2)}) collective-permute-start(bf16[256,512]{1,0:T(8,128)(2,1)S(1)} %get-tuple-element.357), channel_id=1, source_target_pairs={{0,8},{8,0},{16,24},{24,16},{32,40},{40,32},{48,56},{56,48},{64,72... | collective-permute-start | bytes 786440 | tf_op jit(solution)/shard_map/cond/branch_7_fun/ppermute | solution.py:399

commit v2 on v0

v2 whole, which is shorter than its diff:
```python
import functools

import jax
import jax.numpy as jnp
from jax import lax
from jax.experimental import pallas as pl
from jax.experimental.pallas import tpu as pltpu
from jax.sharding import PartitionSpec as P

HD = 128
rope_base = 500000.0
norm_eps = 1e-05
masked = -1e30
log2e = 1.4426950408889634
VMEM_LIMIT = 62 << 20
MESH = pl.DeviceIdType.MESH


def peers():
    n = lax.axis_size("tensor")
    t = lax.axis_index("tensor")
    core = lax.rem(t, 2)
    return t, core, lax.rem(t + 2, n), lax.rem(t + n - 2, n), t + 1 - 2 * core


def greet(devices):
    barrier = pltpu.get_barrier_semaphore()
    for device in devices:
        pl.semaphore_signal(barrier, inc=1, device_id=device, device_id_type=MESH)
    pl.semaphore_wait(barrier, len(devices))


def remote(source, target, sems, index, device):
    return pltpu.make_async_remote_copy(
        src_ref=source,
        dst_ref=target,
        send_sem=sems.at[(0, *index)],
        recv_sem=sems.at[(1, *index)],
        device_id=device,
        device_id_type=MESH,
    )


TO_RIGHT, TO_LEFT, TO_SIB, ONWARD, SIB_LEFT, SIB_RIGHT, SIB_FAR = range(7)
SWAP, FAR, SUM_RIGHT, SUM_LEFT = range(4)
NEIGHBOURS, FAR_BLOCK, PRODUCT = 2, 4, 5
CHIP_SUM, PASS_ON, RESULT = 1, 3, 5


def layer_kernel(
    plan, flags_ref, lengths_ref, x_ref, cos_ref, sin_ref, wq_ref, wk_ref, wv_ref, wo_ref,
    ck_ref, cv_ref, out_ref,
    rows, hop, weights, weights_out, cache_k, cache_v, total, packed, heads, back, home,
    mine, swap_out, swap_in, far_out, far_in, sum_out, sum_in,
    local_sem, near_sem, hop_sem, gather_sem, near_back_sem, back_sem, reduce_sem,
):
    chunks, stages, q_heads = plan
    t, core, right, left, sib = peers()
    n = lax.axis_size("tensor")
    chips = n // 2
    far = lax.rem(t + chips, n)
    z = t // 2
    z_right, z_left, z_far = right // 2, left // 2, far // 2
    d = lax.axis_index("dp")
    block = x_ref.shape[1]
    span_rows = block * n
    width = rows.shape[-1]
    q_width, kv_width = wq_ref.shape[1], wk_ref.shape[1]
    bf16, f32 = jnp.bfloat16, jnp.float32
    total_chunks = 2 * chunks

    def flipped(bit):
        size = 1 << bit
        return {"dp": d + size - 2 * size * lax.rem(d // size, 2)}

    def across(device):
        return {"tensor": device}

    def stage_device(s):
        return flipped(stages - 1 - s)

    def at(device):
        return pl.ds(pl.multiple_of(device * block, block), block)

    def columns(k):
        return pl.ds(pl.multiple_of(k * width, width), width)

    def head_columns(h):
        return pl.ds(pl.multiple_of(h * HD, HD), HD)

    def near(k):
        return remote(
            x_ref.at[0, :, columns(k)], rows.at[0, k, at(t), :], near_sem, (k,), flipped(0)
        )

    def hop_source(s, k):
        return x_ref.at[1, :, columns(k)] if s == 0 else hop.at[s - 1, k]

    def hops(s, k):
        return remote(hop_source(s, k), hop.at[s, k], hop_sem, (s, k), stage_device(s))

    def gather(kind, q, owner, device):
        view = rows.at[q // chunks, lax.rem(q, chunks), at(owner), :]
        return remote(view, view, gather_sem, (kind, q), across(device))

    def onward(q):
        odd = lax.rem(q, 2)
        return gather(
            ONWARD, q, left * (1 - odd) + right * odd, right * (1 - odd) + left * odd
        )

    def near_back(h):
        return remote(
            heads.at[0, :, head_columns(h)], home.at[0, :, head_columns(h)],
            near_back_sem, (h,), flipped(0),
        )

    def back_source(s, h):
        return heads.at[1, :, head_columns(h)] if s == 0 else back.at[s - 1, h]

    def backs(s, h):
        return remote(back_source(s, h), back.at[s, h], back_sem, (s, h), stage_device(s))

    def swap(r):
        return remote(swap_out.at[r], swap_in.at[r], reduce_sem, (SWAP, r), across(sib))

    def far_sum(r):
        odd = lax.rem(r, 2)
        return remote(
            far_out.at[r], far_in.at[r], reduce_sem, (FAR, r),
            across(right * (1 - odd) + left * odd),
        )

    def sum_right(r):
        return remote(
            sum_out.at[r, 0], sum_in.at[r, 0], reduce_sem, (SUM_RIGHT, r), across(right)
        )

    def sum_left(r):
        return remote(
            sum_out.at[r, 1], sum_in.at[r, 1], reduce_sem, (SUM_LEFT, r), across(left)
        )

    def weight_copy(index):
        ref = (wq_ref, wk_ref, wv_ref)[index]
        start = (0, q_width, q_width + kv_width)[index]
        return pltpu.make_async_copy(
            ref, weights.at[:, pl.ds(start, ref.shape[1])], local_sem.at[index]
        )

    def out_copy(j):
        return pltpu.make_async_copy(
            wo_ref.at[:, columns(j)], weights_out.at[j], local_sem.at[5 + j]
        )

    cache_copies = (
        pltpu.make_async_copy(ck_ref, cache_k, local_sem.at[3]),
        pltpu.make_async_copy(cv_ref, cache_v, local_sem.at[4]),
    )

    greet([across(right), across(left), across(sib)] + [flipped(b) for b in range(stages)])
    for k in range(chunks):
        near(k).start()
    for k in range(chunks):
        hops(0, k).start()
    for index in range(3):
        weight_copy(index).start()
    for copy in cache_copies:
        copy.start()
    for j in range(chunks):
        out_copy(j).start()
    total[...] = jnp.zeros_like(total)

    def mix(flag, taken, kept):
        return (taken.astype(f32) * flag + kept.astype(f32) * (1.0 - flag)).astype(bf16)

    sib_of = 1 - 2 * core
    attend_near = chunks + PRODUCT
    attend_other = total_chunks + PRODUCT
    reduce_near = attend_near + q_heads + 1
    reduce_other = max(attend_other + q_heads + stages, reduce_near + chunks)
    last = reduce_other + chunks + RESULT
    contract = (((1,), (1,)), ((), ()))

    def within(value, low, high):
        return (value >= low) & (value < high)

    def reduce_index(tick):
        first = tick - reduce_near
        second = tick - reduce_other
        on_first, on_second = within(first, 0, chunks), within(second, 0, chunks)
        late = lax.select(second >= 0, 1, 0)
        return first * (1 - late) + (second + chunks) * late, on_first | on_second

    def tick_body(tick, carry):
        @pl.when(tick < chunks)
        def _():
            near(tick).wait_recv()

        @pl.when(tick < total_chunks)
        def _():
            gather(TO_RIGHT, tick, t, right).start()
            gather(TO_LEFT, tick, t, left).start()
            gather(TO_SIB, tick, t, sib).start()

        @pl.when(within(tick - NEIGHBOURS, 0, total_chunks))
        def _():
            q = tick - NEIGHBOURS
            gather(TO_RIGHT, q, left, right).wait_recv()
            gather(TO_LEFT, q, right, left).wait_recv()
            onward(q).start()
            gather(SIB_LEFT, q, left, sib).start()
            gather(SIB_RIGHT, q, right, sib).start()

        @pl.when(within(tick - FAR_BLOCK, 0, total_chunks))
        def _():
            q = tick - FAR_BLOCK
            onward(q).wait_recv()
            gather(SIB_FAR, q, far, sib).start()

        for s in range(stages):
            k = tick - (chunks - 2 * stages + 2 * s)

            @pl.when(within(k, 0, chunks))
            def _(s=s, k=k):
                hops(s, k).wait_recv()
                flag = flags_ref[s]
                value = mix(flag, hop[s, k], hop_source(s, k)[...])
                if s < stages - 1:
                    hop[s, k] = value
                    hops(s + 1, k).start()
                else:
                    rows[1, k, at(t), :] = value

        @pl.when(tick == PRODUCT - 1)
        def _():
            for copy in cache_copies:
                copy.wait()
            flag = flags_ref[stages]
            for cache in (cache_k, cache_v):
                first, second = cache[0], cache[1]
                cache[0] = mix(flag, second, first)
                cache[1] = mix(flag, first, second)
            for index in range(3):
                weight_copy(index).wait()

        r, on = reduce_index(tick - PASS_ON)

        @pl.when(on)
        def _():
            odd = lax.rem(r, 2).astype(f32)
            far_sum(r).wait_recv()
            passed = far_in[r].astype(f32)
            sum_out[r, 0] = (mine[r, z_right].astype(f32) + passed * (1.0 - odd)).astype(bf16)
            sum_out[r, 1] = (mine[r, z_left].astype(f32) + passed * odd).astype(bf16)
            sum_right(r).start()
            sum_left(r).start()

        r, on = reduce_index(tick - CHIP_SUM)

        @pl.when(on)
        def _():
            swap(r).wait_recv()
            value = mine[r].astype(f32) + swap_in[r].astype(f32)
            mine[r] = value.astype(bf16)
            far_out[r] = mine[r, z_far]
            far_sum(r).start()

        r, on = reduce_index(tick)

        @pl.when(on)
        def _():
            p, j = r // chunks, lax.rem(r, chunks)

            @pl.when(r == 0)
            def _():
                for h in range(q_heads):
                    near_back(h).wait_recv()

            @pl.when(r < chunks)
            def _():
                out_copy(j).wait()

            part = jnp.dot(home[p], weights_out[j], preferred_element_type=f32)
            part = part.reshape(chips, 2, block, width)
            mine[r] = jnp.where(core == 0, part[:, 0], part[:, 1]).astype(bf16)
            swap_out[r] = jnp.where(core == 0, part[:, 1], part[:, 0]).astype(bf16)
            swap(r).start()

        @pl.when(within(tick - PRODUCT, 0, total_chunks))
        def _():
            q = tick - PRODUCT
            p, k = q // chunks, lax.rem(q, chunks)
            gather(TO_SIB, q, sib, sib).wait_recv()
            gather(SIB_LEFT, q, left + sib_of, sib).wait_recv()
            gather(SIB_RIGHT, q, right + sib_of, sib).wait_recv()
            gather(SIB_FAR, q, far + sib_of, sib).wait_recv()
            total[...] += jnp.dot(rows[p, k], weights[columns(k), :], preferred_element_type=f32)

            @pl.when(k == chunks - 1)
            def _():
                cosine, sine = cos_ref[p], sin_ref[p]
                for h in range((q_width + kv_width) // HD):
                    place = pl.ds(h * HD, HD)
                    value = total[:, place]
                    value = value * cosine + pltpu.roll(value, HD // 2, axis=1) * sine
                    if h < q_heads:
                        value = value * (HD ** (-0.5) * log2e)
                    packed[p, :, place] = value.astype(bf16)
                place = pl.ds(q_width + kv_width, kv_width)
                packed[p, :, place] = total[:, place].astype(bf16)
                total[...] = jnp.zeros_like(total)

        @pl.when(
            within(tick - attend_near, 0, q_heads) | within(tick - attend_other, 0, q_heads)
        )
        def _():
            late = lax.select(tick >= attend_other, 1, 0)
            p = late
            h = tick - attend_near * (1 - late) - attend_other * late
            prefix, span = lengths_ref[p], lengths_ref[2 + p]
            prefix_rows = cache_k.shape[1]
            keys_new = packed[p, :, pl.ds(q_width, kv_width)]
            values_new = packed[p, :, pl.ds(q_width + kv_width, kv_width)]
            old_column = lax.broadcasted_iota(jnp.int32, (1, prefix_rows), 1)
            old_bias = jnp.where(old_column < prefix, 0.0, masked)
            row = lax.broadcasted_iota(jnp.int32, (span_rows, span_rows), 0)
            column = lax.broadcasted_iota(jnp.int32, (span_rows, span_rows), 1)
            new_bias = jnp.where((column <= row) & (column < span), 0.0, masked)
            query = packed[p, :, head_columns(h)]
            old = lax.dot_general(query, cache_k[p], contract, preferred_element_type=f32)
            old = old + old_bias
            new = lax.dot_general(query, keys_new, contract, preferred_element_type=f32)
            new = new + new_bias
            top = jnp.maximum(
                jnp.max(old, axis=1, keepdims=True), jnp.max(new, axis=1, keepdims=True)
            )
            old = jnp.exp2(old - top)
            new = jnp.exp2(new - top)
            weight_sum = jnp.sum(old, axis=1, keepdims=True) + jnp.sum(
                new, axis=1, keepdims=True
            )
            mixed = jnp.dot(old.astype(bf16), cache_v[p], preferred_element_type=f32)
            mixed += jnp.dot(new.astype(bf16), values_new, preferred_element_type=f32)
            heads[p, :, head_columns(h)] = (mixed / weight_sum).astype(bf16)

            @pl.when(p == 0)
            def _():
                near_back(h).start()

            @pl.when(p == 1)
            def _():
                backs(0, h).start()

        for s in range(stages):
            h = tick - (attend_other + 1 + s)

            @pl.when(within(h, 0, q_heads))
            def _(s=s, h=h):
                backs(s, h).wait_recv()
                value = mix(flags_ref[s], back[s, h], back_source(s, h)[...])
                if s < stages - 1:
                    back[s, h] = value
                    backs(s + 1, h).start()
                else:
                    home[1, :, head_columns(h)] = value

        r, on = reduce_index(tick - RESULT)

        @pl.when(on)
        def _():
            p, j = r // chunks, lax.rem(r, chunks)
            sum_right(r).wait_recv()
            sum_left(r).wait_recv()
            out_ref[p, :, columns(j)] = (
                mine[r, z].astype(f32) + sum_in[r, 0].astype(f32) + sum_in[r, 1].astype(f32)
            ).astype(bf16)

        return carry

    lax.fori_loop(0, last, tick_body, 0)

    def drain_rows(k, carry):
        near(k).wait_send()
        for s in range(stages):
            hops(s, k).wait_send()
        return carry

    def drain_blocks(q, carry):
        gather(TO_RIGHT, q, t, right).wait_send()
        gather(TO_LEFT, q, t, left).wait_send()
        gather(TO_SIB, q, t, sib).wait_send()
        onward(q).wait_send()
        gather(SIB_LEFT, q, left, sib).wait_send()
        gather(SIB_RIGHT, q, right, sib).wait_send()
        gather(SIB_FAR, q, far, sib).wait_send()
        swap(q).wait_send()
        far_sum(q).wait_send()
        sum_right(q).wait_send()
        sum_left(q).wait_send()
        return carry

    def drain_heads(h, carry):
        near_back(h).wait_send()
        for s in range(stages):
            backs(s, h).wait_send()
        return carry

    lax.fori_loop(0, chunks, drain_rows, 0)
    lax.fori_loop(0, total_chunks, drain_blocks, 0)
    lax.fori_loop(0, q_heads, drain_heads, 0)


def layer(flags, lengths, x, cosine, sine, wq, wk, wv, wo, cache_keys, cache_values, chunks=8):
    packets, block, depth = x.shape
    n, dp = lax.axis_size("tensor"), lax.axis_size("dp")
    stages = dp.bit_length() - 1
    q_width, kv_width = wq.shape[1], wk.shape[1]
    all_width = q_width + 2 * kv_width
    q_heads = q_width // HD
    rows, width = block * n, depth // chunks
    bf16, f32 = jnp.bfloat16, jnp.float32
    any_space = pl.BlockSpec(memory_space=pl.ANY)
    smem = pl.BlockSpec(memory_space=pltpu.SMEM)
    vmem = pl.BlockSpec(memory_space=pltpu.VMEM)
    steps = packets * chunks
    dma = pltpu.SemaphoreType.DMA
    return pl.pallas_call(
        functools.partial(layer_kernel, (chunks, stages, q_heads)),
        out_shape=jax.ShapeDtypeStruct((packets, block, depth), bf16),
        in_specs=[smem] * 2 + [vmem] * 3 + [any_space] * 6,
        out_specs=vmem,
        scratch_shapes=[
            pltpu.VMEM((packets, chunks, rows, width), bf16),
            pltpu.VMEM((stages, chunks, block, width), bf16),
            pltpu.VMEM((depth, all_width), bf16),
            pltpu.VMEM((chunks, q_width, width), bf16),
            pltpu.VMEM(cache_keys.shape, bf16),
            pltpu.VMEM(cache_values.shape, bf16),
            pltpu.VMEM((rows, all_width), f32),
            pltpu.VMEM((packets, rows, all_width), bf16),
            pltpu.VMEM((packets, rows, q_width), bf16),
            pltpu.VMEM((stages, q_heads, rows, HD), bf16),
            pltpu.VMEM((packets, rows, q_width), bf16),
            pltpu.VMEM((steps, n // 2, block, width), bf16),
            pltpu.VMEM((steps, n // 2, block, width), bf16),
            pltpu.VMEM((steps, n // 2, block, width), bf16),
            pltpu.VMEM((steps, block, width), bf16),
            pltpu.VMEM((steps, block, width), bf16),
            pltpu.VMEM((steps, 2, block, width), bf16),
            pltpu.VMEM((steps, 2, block, width), bf16),
            dma((5 + chunks,)),
            dma((2, chunks)),
            dma((2, stages, chunks)),
            dma((2, 7, steps)),
            dma((2, q_heads)),
            dma((2, stages, q_heads)),
            dma((2, 4, steps)),
        ],
        compiler_params=pltpu.CompilerParams(
            collective_id=0, has_side_effects=True, vmem_limit_bytes=VMEM_LIMIT
        ),
        name="layer",
    )(flags, lengths, x, cosine, sine, wq, wk, wv, wo, cache_keys, cache_values)


def local(
    hidden_rows, norm_gain, w_query, w_key, w_value, w_out, cache_keys, cache_values,
    slot_of_request, span_length, prefix_length,
):
    per_device = hidden_rows.shape[1]
    data_index = lax.axis_index("dp")
    span_rows = hidden_rows.shape[0] * lax.axis_size("tensor")
    stages = lax.axis_size("dp").bit_length() - 1
    ids = jnp.arange(per_device, dtype=jnp.int32) + data_index * per_device
    requests = jnp.arange(slot_of_request.shape[0], dtype=jnp.int32)
    mine = jnp.sum(jnp.where(requests[None, :] == ids[:, None], slot_of_request[None, :], 0), axis=1)
    masks = jnp.bitwise_xor(mine // per_device, data_index)
    flip = masks[0] != 1
    mask = jnp.where(flip, masks[0], masks[1])
    match = slot_of_request[None, :] == ids[:, None]
    request_of = jnp.sum(jnp.where(match, requests[None, :], 0), axis=1)
    slot_prefix = jnp.sum(jnp.where(match, prefix_length[None, :], 0), axis=1)
    slot_span = jnp.sum(jnp.where(match, span_length[None, :], 0), axis=1)
    swapped = jnp.bitwise_xor(request_of[0] // per_device, data_index) != 1
    prefix = jnp.where(swapped, slot_prefix[::-1], slot_prefix)
    span = jnp.where(swapped, slot_span[::-1], slot_span)
    bits = (mask // 2 ** (stages - 1 - jnp.arange(stages, dtype=jnp.int32))) % 2
    flags = jnp.concatenate([bits, swapped.astype(jnp.int32)[None]]).astype(jnp.float32)
    lengths = jnp.concatenate([prefix, span])

    floats = hidden_rows.astype(jnp.float32)
    normed = (
        floats * lax.rsqrt(jnp.mean(floats * floats, axis=-1, keepdims=True) + norm_eps) * norm_gain
    ).astype(jnp.bfloat16)
    normed = jnp.transpose(jnp.where(flip, normed[:, ::-1], normed), (1, 0, 2))

    frequency = rope_base ** (-(jnp.arange(HD // 2, dtype=jnp.float32) * 2.0 / HD))
    positions = (prefix[:, None] + jnp.arange(span_rows, dtype=jnp.int32)[None, :]).astype(
        jnp.float32
    )
    angles = positions[:, :, None] * frequency
    cosine, sine = jnp.cos(angles), jnp.sin(angles)
    cosine = jnp.concatenate([cosine, cosine], axis=-1)
    sine = jnp.concatenate([-sine, sine], axis=-1)
    result = layer(
        flags, lengths, normed, cosine, sine, w_query, w_key, w_value, w_out,
        cache_keys, cache_values,
    )
    return jnp.transpose(jnp.where(flip, result[::-1], result), (1, 0, 2))


def solution(mesh):
    placed = (
        P("tensor", "dp", None),
        P(),
        P(None, "tensor"),
        P(None, "tensor"),
        P(None, "tensor"),
        P("tensor", None),
        P("dp", None, "tensor"),
        P("dp", None, "tensor"),
        P(),
        P(),
        P(),
    )
    return jax.shard_map(
        local, mesh=mesh, in_specs=placed, out_specs=P("tensor", "dp", None), check_vma=False
    )
```

time: 449 us -> 140 us (0.31); the launches traced: 442 us -> 140 us
  waiting for transfers between devices: 249 us -> 0 us
  Pallas kernels: 0 us -> 124 us
  matrix products: 86.9 us -> 0 us
  blocking collectives: 56 us -> 0 us
  local copies, waits for them, and re-layouts: 19 us -> 2.91 us
  between operations: 14 us -> 2.05 us
  starting transfers between devices: 8.49 us -> 0 us
    all_to_all x1 -> x0, waiting for transfers between devices: 145 us -> none  [local(): lax.all_to_all(outgoing, 'dp', split_axis=0, concat_axis=0, tiled=True)]
    pallas_call x0 -> x1, Pallas kernels: none -> 124 us  [layer(): pl.pallas_call(functools.partial(layer_kernel, (chunks, stages, q_heads))...]
    dot_general x11 -> x0, matrix products: 86.9 us -> none  [the longest x1 14.5 us: attend_slots(): jnp.einsum('sgmcj,jsgd->csgmd', weight_new, values_new, preferred_element...]
    all_to_all x1 -> x0, blocking collectives: 56 us -> none  [local(): lax.all_to_all(outgoing_back, 'dp', split_axis=0, concat_axis=0, tiled=True)]
    all_gather x1 -> x0, waiting for transfers between devices: 53.7 us -> none  [project_group(): piece_rows = lax.all_gather(normed, 'tensor', axis=0, tiled=True)]
    reduce_scatter x1 -> x0, waiting for transfers between devices: 50.2 us -> none  [local(): lax.psum_scatter(jnp.dot(flat_heads, w_out, preferred_element_type=jnp.fl...]
    convert_element_type x3 -> x0, local copies, waits for them, and re-layouts: 16.1 us -> none  [the longest x1 11.2 us: local(): outgoing = jnp.einsum('js,csf->jcf', send_table, normed, preferred_elemen...]
    all_to_all x1 -> x0, starting transfers between devices: 7.77 us -> none  [local(): lax.all_to_all(outgoing, 'dp', split_axis=0, concat_axis=0, tiled=True)]
  transfers between devices with their start and end apart: 3 -> 0, of which waited for: 3 -> 0; matrix products, arithmetic and copies ran while one was open for 1% -> 0% of each run, Pallas kernels for 0% -> 0%
where the time goes in v2:
time: 140 us
  Pallas kernels  124 us (89%)
  other arithmetic  11.2 us (8%)
  local copies, waits for them, and re-layouts  2.91 us (2%)
  between operations  2.05 us (1%)
    pallas_call x1, Pallas kernels, layer(): pl.pallas_call(functools.partial(layer_kernel, (chunks, stages, q_heads))...  124 us

profile of v2, /device:TPU:1, one launch (start us, length us, event | category | flops | bytes accessed | tf_op | source)
XLA Modules:
  0.0 140.2 jit_solution(16402057392446269133)
XLA Ops:
  0.0 0.0 copy-start
  0.0 0.0 copy-start.1
  0.0 2.5 %fusion = f32[32,2]{0,1:T(2,128)S(1)} fusion(bf16[32,2,8192]{2,1,0:T(2,128)(2,1)} %param.11), kind=kLoop, calls=%fused_computation.2 | loop fusion | flops 1572800 | bytes 1048832 | tf_op jit(solution)/shard_map/reduce_sum | solution.py:494
  2.5 0.9 fusion.8
  3.6 0.1 rev.12
  3.7 0.1 rev.13
  3.8 0.6 pad_add_fusion.lengths_ref
  4.4 0.7 fusion.12
  6.9 0.1 and_select_fusion
  7.1 0.7 add_convert_fusion.1.flags_ref
  7.7 0.1 add_convert_fusion
  7.8 1.0 fusion.5
  8.8 0.9 pad_maximum_fusion.1.sin_ref
  9.6 0.9 pad_maximum_fusion.cos_ref
  10.5 0.0 copy-done
  10.5 0.0 copy-done.1
  10.5 0.6 fusion.2
  11.1 1.1 fusion.3.x_ref
  12.3 124.0 %layer.1 = bf16[2,32,8192]{2,1,0:T(8,128)(2,1)} custom-call(f32[5]{0:T(128)} %add_convert_fusion.1.flags_ref, s32[4]{0:T(128)} %pad_add_fusion.lengths_ref, bf16[2,32,8192]{2,1,0:T(8,128)(2,1)} %fusion.3.x_ref, f32[2,256,128]{2,1,0:T(8,128)} %pad_maximum_fusion.cos_ref, f32[2,256,128]{2,1,0:T(8,128)} %pad_maximum_fusion.1.sin_ref, bf16[8192,512]{1,0:T(8,128)(2,1)} %wq_ref.1, ...), custom_call_target="tpu_custom_call" | custom-call | tf_op jit(solution)/shard_map/layer/pallas_call | solution.py:428
  136.3 1.8 %fusion.4 = bf16[32,2,8192]{2,0,1:T(8,128)(2,1)S(1)} fusion(bf16[2,32,8192]{2,1,0:T(8,128)(2,1)} %layer.1, pred[]{:T(512)S(6)} %ne.92), kind=kLoop, calls=%fused_computation.8 | loop fusion | flops 524288 | bytes 2097153 | tf_op jit(solution)/shard_map/transpose | solution.py:510
  138.1 2.1 %copy.15 = bf16[32,2,8192]{2,1,0:T(2,128)(2,1)} copy(bf16[32,2,8192]{2,0,1:T(8,128)(2,1)S(1)} %fusion.4) | data formatting | bytes 2097152 | tf_op jit(solution)/shard_map/transpose | solution.py:510
  (5 shorter events, 0.0 us)
Async XLA Ops:
  0.0 10.5 %copy-start = (bf16[32,2,8192]{2,1,0:T(2,128)(2,1)S(1)}, bf16[32,2,8192]{2,1,0:T(2,128)(2,1)}, u32[]{:S(2)}) copy-start(bf16[32,2,8192]{2,1,0:T(2,128)(2,1)} %param.11) | copy-start | bytes 3145732
  0.0 10.5 %copy-start.1 = (f32[8192]{0:T(1024)S(1)}, f32[8192]{0:T(1024)}, u32[]{:S(2)}) copy-start(f32[8192]{0:T(1024)} %param.12) | copy-start | bytes 98308

commit v3 on v2

--- a/solution.py
+++ b/solution.py
@@ -2,6 +2,7 @@
 
 import jax
 import jax.numpy as jnp
+import numpy as np
 from jax import lax
 from jax.experimental import pallas as pl
 from jax.experimental.pallas import tpu as pltpu
@@ -45,16 +46,18 @@
 SWAP, FAR, SUM_RIGHT, SUM_LEFT = range(4)
 NEIGHBOURS, FAR_BLOCK, PRODUCT = 2, 4, 5
 CHIP_SUM, PASS_ON, RESULT = 1, 3, 5
+ROWS_FIRST, ROWS_SECOND = 3, 7
+HEAD_FIRST, HEAD_SECOND = 2, 4
 
 
 def layer_kernel(
-    plan, flags_ref, lengths_ref, x_ref, cos_ref, sin_ref, wq_ref, wk_ref, wv_ref, wo_ref,
-    ck_ref, cv_ref, out_ref,
-    rows, hop, weights, weights_out, cache_k, cache_v, total, packed, heads, back, home,
-    mine, swap_out, swap_in, far_out, far_in, sum_out, sum_in,
+    plan, flags_ref, lengths_ref, x_ref, cos_ref, sin_ref, frequency_ref,
+    wq_ref, wk_ref, wv_ref, wo_ref, ck_ref, cv_ref, out_ref,
+    rows, ordered, hop, hopped, weights, weights_out, cache_k, cache_v, total, packed, heads,
+    back, backed, home, mine, swap_out, swap_in, far_out, far_in, sum_out, sum_in,
     local_sem, near_sem, hop_sem, gather_sem, near_back_sem, back_sem, reduce_sem,
 ):
-    chunks, stages, q_heads = plan
+    chunks, stage_bits, q_heads = plan
     t, core, right, left, sib = peers()
     n = lax.axis_size("tensor")
     chips = n // 2
@@ -69,15 +72,21 @@
     bf16, f32 = jnp.bfloat16, jnp.float32
     total_chunks = 2 * chunks
 
-    def flipped(bit):
-        size = 1 << bit
-        return {"dp": d + size - 2 * size * lax.rem(d // size, 2)}
+    def flipped(mask):
+        other = d
+        for bit in range(mask.bit_length()):
+            size = 1 << bit
+            if mask & size:
+                other = other + size - 2 * size * lax.rem(d // size, 2)
+        return {"dp": other}
 
     def across(device):
         return {"tensor": device}
 
-    def stage_device(s):
-        return flipped(stages - 1 - s)
+    stage_masks = (
+        [i << stage_bits[1] for i in range(1, 1 << stage_bits[0])],
+        list(range(1, 1 << stage_bits[1])),
+    )
 
     def at(device):
         return pl.ds(pl.multiple_of(device * block, block), block)
@@ -90,14 +99,16 @@
 
     def near(k):
         return remote(
-            x_ref.at[0, :, columns(k)], rows.at[0, k, at(t), :], near_sem, (k,), flipped(0)
+            ordered.at[0, k], rows.at[0, k, at(t), :], near_sem, (k,), flipped(1)
         )
 
     def hop_source(s, k):
-        return x_ref.at[1, :, columns(k)] if s == 0 else hop.at[s - 1, k]
-
-    def hops(s, k):
-        return remote(hop_source(s, k), hop.at[s, k], hop_sem, (s, k), stage_device(s))
+        return ordered.at[1, k] if s == 0 else hopped.at[k]
+
+    def hops(s, i, k):
+        return remote(
+            hop_source(s, k), hop.at[s, i, k], hop_sem, (s, i, k), flipped(stage_masks[s][i])
+        )
 
     def gather(kind, q, owner, device):
         view = rows.at[q // chunks, lax.rem(q, chunks), at(owner), :]
@@ -112,14 +123,16 @@
     def near_back(h):
         return remote(
             heads.at[0, :, head_columns(h)], home.at[0, :, head_columns(h)],
-            near_back_sem, (h,), flipped(0),
+            near_back_sem, (h,), flipped(1),
         )
 
     def back_source(s, h):
-        return heads.at[1, :, head_columns(h)] if s == 0 else back.at[s - 1, h]
-
-    def backs(s, h):
-        return remote(back_source(s, h), back.at[s, h], back_sem, (s, h), stage_device(s))
+        return heads.at[1, :, head_columns(h)] if s == 0 else backed.at[h]
+
+    def backs(s, i, h):
+        return remote(
+            back_source(s, h), back.at[s, i, h], back_sem, (s, i, h), flipped(stage_masks[s][i])
+        )
 
     def swap(r):
         return remote(swap_out.at[r], swap_in.at[r], reduce_sem, (SWAP, r), across(sib))
@@ -158,11 +171,37 @@
         pltpu.make_async_copy(cv_ref, cache_v, local_sem.at[4]),
     )
 
-    greet([across(right), across(left), across(sib)] + [flipped(b) for b in range(stages)])
-    for k in range(chunks):
+    greet(
+        [across(right), across(left), across(sib)]
+        + [flipped(m) for masks in stage_masks for m in masks]
+    )
+
+    def flip_flags():
+        return flags_ref[0], 1.0 - flags_ref[0]
+
+    def swap_flags():
+        return flags_ref[1], 1.0 - flags_ref[1]
+
+    def keep(s):
+        first = 2 + s * (1 << stage_bits[0])
+        return tuple(flags_ref[first + i] for i in range(1 << stage_bits[s]))
+
+    def mix(parts, flags):
+        value = parts[0].astype(f32) * flags[0]
+        for part, flag in zip(parts[1:], flags[1:]):
+            value = value + part.astype(f32) * flag
+        return value.astype(bf16)
+
+    def order_rows(k, carry):
+        first, second = x_ref[0, :, columns(k)], x_ref[1, :, columns(k)]
+        ordered[0, k] = mix((second, first), flip_flags())
         near(k).start()
-    for k in range(chunks):
-        hops(0, k).start()
+        ordered[1, k] = mix((first, second), flip_flags())
+        for i in range(len(stage_masks[0])):
+            hops(0, i, k).start()
+        return carry
+
+    lax.fori_loop(0, chunks, order_rows, 0)
     for index in range(3):
         weight_copy(index).start()
     for copy in cache_copies:
@@ -171,14 +210,11 @@
         out_copy(j).start()
     total[...] = jnp.zeros_like(total)
 
-    def mix(flag, taken, kept):
-        return (taken.astype(f32) * flag + kept.astype(f32) * (1.0 - flag)).astype(bf16)
-
     sib_of = 1 - 2 * core
     attend_near = chunks + PRODUCT
     attend_other = total_chunks + PRODUCT
     reduce_near = attend_near + q_heads + 1
-    reduce_other = max(attend_other + q_heads + stages, reduce_near + chunks)
+    reduce_other = max(attend_other + q_heads + HEAD_SECOND, reduce_near + chunks)
     last = reduce_other + chunks + RESULT
     contract = (((1,), (1,)), ((), ()))
 
@@ -218,17 +254,19 @@
             onward(q).wait_recv()
             gather(SIB_FAR, q, far, sib).start()
 
-        for s in range(stages):
-            k = tick - (chunks - 2 * stages + 2 * s)
-
-            @pl.when(within(k, 0, chunks))
-            def _(s=s, k=k):
-                hops(s, k).wait_recv()
-                flag = flags_ref[s]
-                value = mix(flag, hop[s, k], hop_source(s, k)[...])
-                if s < stages - 1:
-                    hop[s, k] = value
-                    hops(s + 1, k).start()
+        for s, lag in enumerate((ROWS_FIRST, ROWS_SECOND)):
+
+            @pl.when(within(tick - lag, 0, chunks))
+            def _(s=s, k=tick - lag):
+                found = [hop_source(s, k)[...]]
+                for i in range(len(stage_masks[s])):
+                    hops(s, i, k).wait_recv()
+                    found.append(hop[s, i, k])
+                value = mix(found, keep(s))
+                if s == 0:
+                    hopped[k] = value
+                    for i in range(len(stage_masks[1])):
+                        hops(1, i, k).start()
                 else:
                     rows[1, k, at(t), :] = value
 
@@ -236,11 +274,10 @@
         def _():
             for copy in cache_copies:
                 copy.wait()
-            flag = flags_ref[stages]
             for cache in (cache_k, cache_v):
                 first, second = cache[0], cache[1]
-                cache[0] = mix(flag, second, first)
-                cache[1] = mix(flag, first, second)
+                cache[0] = mix((second, first), swap_flags())
+                cache[1] = mix((first, second), swap_flags())
             for index in range(3):
                 weight_copy(index).wait()
 
@@ -299,7 +336,13 @@
 
             @pl.when(k == chunks - 1)
             def _():
-                cosine, sine = cos_ref[p], sin_ref[p]
+                prefix = lengths_ref[p]
+                angle = frequency_ref[...] * prefix.astype(f32)
+                base_cos, base_sin = jnp.cos(angle)[0:1], jnp.sin(angle)[0:1]
+                cosine = cos_ref[...] * base_cos - sin_ref[...] * base_sin
+                sine = sin_ref[...] * base_cos + cos_ref[...] * base_sin
+                lane = lax.broadcasted_iota(jnp.int32, sine.shape, 1)
+                sine = jnp.where(lane < HD // 2, -sine, sine)
                 for h in range((q_width + kv_width) // HD):
                     place = pl.ds(h * HD, HD)
                     value = total[:, place]
@@ -350,18 +393,22 @@
 
             @pl.when(p == 1)
             def _():
-                backs(0, h).start()
-
-        for s in range(stages):
-            h = tick - (attend_other + 1 + s)
-
-            @pl.when(within(h, 0, q_heads))
-            def _(s=s, h=h):
-                backs(s, h).wait_recv()
-                value = mix(flags_ref[s], back[s, h], back_source(s, h)[...])
-                if s < stages - 1:
-                    back[s, h] = value
-                    backs(s + 1, h).start()
+                for i in range(len(stage_masks[0])):
+                    backs(0, i, h).start()
+
+        for s, lag in enumerate((HEAD_FIRST, HEAD_SECOND)):
+
+            @pl.when(within(tick - attend_other - lag, 0, q_heads))
+            def _(s=s, h=tick - attend_other - lag):
+                found = [back_source(s, h)[...]]
+                for i in range(len(stage_masks[s])):
+                    backs(s, i, h).wait_recv()
+                    found.append(back[s, i, h])
+                value = mix(found, keep(s))
+                if s == 0:
+                    backed[h] = value
+                    for i in range(len(stage_masks[1])):
+                        backs(1, i, h).start()
                 else:
                     home[1, :, head_columns(h)] = value
 
@@ -372,18 +419,29 @@
             p, j = r // chunks, lax.rem(r, chunks)
             sum_right(r).wait_recv()
             sum_left(r).wait_recv()
-            out_ref[p, :, columns(j)] = (
+            value = (
                 mine[r, z].astype(f32) + sum_in[r, 0].astype(f32) + sum_in[r, 1].astype(f32)
             ).astype(bf16)
 
+            @pl.when(p == 0)
+            def _():
+                out_ref[0, :, columns(j)] = value
+
+            @pl.when(p == 1)
+            def _():
+                first = out_ref[0, :, columns(j)]
+                out_ref[0, :, columns(j)] = mix((value, first), flip_flags())
+                out_ref[1, :, columns(j)] = mix((first, value), flip_flags())
+
         return carry
 
     lax.fori_loop(0, last, tick_body, 0)
 
     def drain_rows(k, carry):
         near(k).wait_send()
-        for s in range(stages):
-            hops(s, k).wait_send()
+        for s in range(2):
+            for i in range(len(stage_masks[s])):
+                hops(s, i, k).wait_send()
         return carry
 
     def drain_blocks(q, carry):
@@ -402,8 +460,9 @@
 
     def drain_heads(h, carry):
         near_back(h).wait_send()
-        for s in range(stages):
-            backs(s, h).wait_send()
+        for s in range(2):
+            for i in range(len(stage_masks[s])):
+                backs(s, i, h).wait_send()
         return carry
 
     lax.fori_loop(0, chunks, drain_rows, 0)
@@ -411,10 +470,12 @@
     lax.fori_loop(0, q_heads, drain_heads, 0)
 
 
-def layer(flags, lengths, x, cosine, sine, wq, wk, wv, wo, cache_keys, cache_values, chunks=8):
+def layer(flags, lengths, x, cosine, sine, frequency, wq, wk, wv, wo, cache_keys, cache_values, chunks=8):
     packets, block, depth = x.shape
     n, dp = lax.axis_size("tensor"), lax.axis_size("dp")
-    stages = dp.bit_length() - 1
+    low_bits = (dp.bit_length() - 1) // 2
+    stage_bits = (dp.bit_length() - 1 - low_bits, low_bits)
+    most = max((1 << b) - 1 for b in stage_bits)
     q_width, kv_width = wq.shape[1], wk.shape[1]
     all_width = q_width + 2 * kv_width
     q_heads = q_width // HD
@@ -426,13 +487,15 @@
     steps = packets * chunks
     dma = pltpu.SemaphoreType.DMA
     return pl.pallas_call(
-        functools.partial(layer_kernel, (chunks, stages, q_heads)),
+        functools.partial(layer_kernel, (chunks, stage_bits, q_heads)),
         out_shape=jax.ShapeDtypeStruct((packets, block, depth), bf16),
-        in_specs=[smem] * 2 + [vmem] * 3 + [any_space] * 6,
+        in_specs=[smem] * 2 + [vmem] * 4 + [any_space] * 6,
         out_specs=vmem,
         scratch_shapes=[
             pltpu.VMEM((packets, chunks, rows, width), bf16),
-            pltpu.VMEM((stages, chunks, block, width), bf16),
+            pltpu.VMEM((packets, chunks, block, width), bf16),
+            pltpu.VMEM((2, most, chunks, block, width), bf16),
+            pltpu.VMEM((chunks, block, width), bf16),
             pltpu.VMEM((depth, all_width), bf16),
             pltpu.VMEM((chunks, q_width, width), bf16),
             pltpu.VMEM(cache_keys.shape, bf16),
@@ -440,7 +503,8 @@
             pltpu.VMEM((rows, all_width), f32),
             pltpu.VMEM((packets, rows, all_width), bf16),
             pltpu.VMEM((packets, rows, q_width), bf16),
-            pltpu.VMEM((stages, q_heads, rows, HD), bf16),
+            pltpu.VMEM((2, most, q_heads, rows, HD), bf16),
+            pltpu.VMEM((q_heads, rows, HD), bf16),
             pltpu.VMEM((packets, rows, q_width), bf16),
             pltpu.VMEM((steps, n // 2, block, width), bf16),
             pltpu.VMEM((steps, n // 2, block, width), bf16),
@@ -451,63 +515,64 @@
             pltpu.VMEM((steps, 2, block, width), bf16),
             dma((5 + chunks,)),
             dma((2, chunks)),
-            dma((2, stages, chunks)),
+            dma((2, 2, most, chunks)),
             dma((2, 7, steps)),
             dma((2, q_heads)),
-            dma((2, stages, q_heads)),
+            dma((2, 2, most, q_heads)),
             dma((2, 4, steps)),
         ],
         compiler_params=pltpu.CompilerParams(
             collective_id=0, has_side_effects=True, vmem_limit_bytes=VMEM_LIMIT
         ),
         name="layer",
-    )(flags, lengths, x, cosine, sine, wq, wk, wv, wo, cache_keys, cache_values)
+    )(flags, lengths, x, cosine, sine, frequency, wq, wk, wv, wo, cache_keys, cache_values)
 
 
 def local(
     hidden_rows, norm_gain, w_query, w_key, w_value, w_out, cache_keys, cache_values,
     slot_of_request, span_length, prefix_length,
 ):
+    span_rows = hidden_rows.shape[0] * lax.axis_size("tensor")
     per_device = hidden_rows.shape[1]
     data_index = lax.axis_index("dp")
-    span_rows = hidden_rows.shape[0] * lax.axis_size("tensor")
-    stages = lax.axis_size("dp").bit_length() - 1
+    low = 1 << ((lax.axis_size("dp").bit_length() - 1) // 2)
+    high = lax.axis_size("dp") // low
     ids = jnp.arange(per_device, dtype=jnp.int32) + data_index * per_device
     requests = jnp.arange(slot_of_request.shape[0], dtype=jnp.int32)
-    mine = jnp.sum(jnp.where(requests[None, :] == ids[:, None], slot_of_request[None, :], 0), axis=1)
-    masks = jnp.bitwise_xor(mine // per_device, data_index)
+    mine = requests[None, :] == ids[:, None]
+    masks = jnp.bitwise_xor(
+        jnp.sum(jnp.where(mine, slot_of_request[None, :], 0), axis=1) // per_device, data_index
+    )
     flip = masks[0] != 1
     mask = jnp.where(flip, masks[0], masks[1])
     match = slot_of_request[None, :] == ids[:, None]
-    request_of = jnp.sum(jnp.where(match, requests[None, :], 0), axis=1)
-    slot_prefix = jnp.sum(jnp.where(match, prefix_length[None, :], 0), axis=1)
-    slot_span = jnp.sum(jnp.where(match, span_length[None, :], 0), axis=1)
-    swapped = jnp.bitwise_xor(request_of[0] // per_device, data_index) != 1
-    prefix = jnp.where(swapped, slot_prefix[::-1], slot_prefix)
-    span = jnp.where(swapped, slot_span[::-1], slot_span)
-    bits = (mask // 2 ** (stages - 1 - jnp.arange(stages, dtype=jnp.int32))) % 2
-    flags = jnp.concatenate([bits, swapped.astype(jnp.int32)[None]]).astype(jnp.float32)
-    lengths = jnp.concatenate([prefix, span])
-
+    near = jnp.bitwise_xor(requests // per_device, data_index) == 1
+    swapped = ~jnp.any(match[0] & near)
+    packet = jnp.stack([jnp.where(swapped, match[1], match[0]), jnp.where(swapped, match[0], match[1])])
+    lengths = jnp.sum(
+        jnp.where(packet[None], jnp.stack([prefix_length, span_length])[:, None, :], 0), axis=-1
+    ).reshape(-1)
+    flags = jnp.concatenate(
+        [
+            flip[None], swapped[None],
+            mask // low == jnp.arange(high, dtype=jnp.int32),
+            mask % low == jnp.arange(low, dtype=jnp.int32),
+        ]
+    ).astype(jnp.float32)
     floats = hidden_rows.astype(jnp.float32)
     normed = (
         floats * lax.rsqrt(jnp.mean(floats * floats, axis=-1, keepdims=True) + norm_eps) * norm_gain
     ).astype(jnp.bfloat16)
-    normed = jnp.transpose(jnp.where(flip, normed[:, ::-1], normed), (1, 0, 2))
-
-    frequency = rope_base ** (-(jnp.arange(HD // 2, dtype=jnp.float32) * 2.0 / HD))
-    positions = (prefix[:, None] + jnp.arange(span_rows, dtype=jnp.int32)[None, :]).astype(
-        jnp.float32
-    )
-    angles = positions[:, :, None] * frequency
-    cosine, sine = jnp.cos(angles), jnp.sin(angles)
-    cosine = jnp.concatenate([cosine, cosine], axis=-1)
-    sine = jnp.concatenate([-sine, sine], axis=-1)
+    half = rope_base ** (-(np.arange(HD // 2, dtype=np.float64) * 2.0 / HD))
+    frequency = np.concatenate([half, half])
+    angles = np.arange(span_rows, dtype=np.float64)[:, None] * frequency
     result = layer(
-        flags, lengths, normed, cosine, sine, w_query, w_key, w_value, w_out,
-        cache_keys, cache_values,
-    )
-    return jnp.transpose(jnp.where(flip, result[::-1], result), (1, 0, 2))
+        flags, lengths, jnp.transpose(normed, (1, 0, 2)),
+        jnp.asarray(np.cos(angles), jnp.float32), jnp.asarray(np.sin(angles), jnp.float32),
+        jnp.asarray(np.broadcast_to(frequency, (8, HD)), jnp.float32),
+        w_query, w_key, w_value, w_out, cache_keys, cache_values,
+    )
+    return jnp.transpose(result, (1, 0, 2))
 
 
 def solution(mesh):

time: 140 us -> 130 us (0.929)
  Pallas kernels: 124 us -> 114 us
  other arithmetic: 11.2 us -> 9 us
  local copies, waits for them, and re-layouts: 2.91 us -> 4.47 us
    pallas_call x1, Pallas kernels: 124 us -> 114 us  [layer(): pl.pallas_call(functools.partial(layer_kernel, (chunks, stage_bits, q_hea...]
    concatenate x3 -> x0, other arithmetic: 2.33 us -> none  [the longest x1 0.86 us: local(): sine = jnp.concatenate([-sine, sine], axis=-1)]
    transpose x2 -> x1, other arithmetic: 2.94 us -> 2.85 us  [local(): jnp.transpose(normed, (1, 0, 2))]
where the time goes in v3:
time: 130 us
  Pallas kernels  114 us (88%)
  other arithmetic  9 us (7%)
  local copies, waits for them, and re-layouts  4.47 us (3%)
  between operations  2.63 us (2%)
    pallas_call x1, Pallas kernels, layer(): pl.pallas_call(functools.partial(layer_kernel, (chunks, stage_bits, q_hea...  114 us
    transpose x1, local copies, waits for them, and re-layouts, local(): return jnp.transpose(result, (1, 0, 2))  3.28 us
    transpose x1, other arithmetic, local(): jnp.transpose(normed, (1, 0, 2))  2.85 us

profile of v3, /device:TPU:1, one launch (start us, length us, event | category | flops | bytes accessed | tf_op | source)
XLA Modules:
  0.0 130.0 jit_solution(15436308053039212414)
XLA Ops:
  0.0 0.7 broadcast_compare_fusion
  0.7 0.6 fusion.4
  2.0 0.8 fusion.5
  2.9 0.6 fusion.8
  5.4 0.7 add_convert_fusion.flags_ref
  6.1 0.7 pad_add_fusion.1
  6.8 0.1 select_reduce_fusion
  6.9 0.6 reshape.19.lengths_ref
  7.5 2.4 %fusion = f32[32,2]{0,1:T(2,128)S(1)} fusion(bf16[32,2,8192]{2,1,0:T(2,128)(2,1)} %param.14), kind=kLoop, calls=%fused_computation.2 | loop fusion | flops 1572800 | bytes 1048832 | tf_op jit(solution)/shard_map/reduce_sum | solution.py:564
  10.0 2.9 %fusion.3.x_ref = bf16[2,32,8192]{2,1,0:T(8,128)(2,1)} fusion(f32[8192]{0:T(1024)} %param.15, f32[32,2]{0,1:T(2,128)S(1)} %add_rsqrt_fusion, bf16[32,2,8192]{2,1,0:T(2,128)(2,1)} %param.14), kind=kLoop, calls=%fused_computation.5 | loop fusion | flops 2097152 | bytes 2130176 | tf_op jit(solution)/shard_map/transpose | solution.py:570
  12.8 113.9 %layer.1 = bf16[2,32,8192]{2,1,0:T(8,128)(2,1)} custom-call(f32[10]{0:T(128)} %add_convert_fusion.flags_ref, s32[4]{0:T(128)} %reshape.19.lengths_ref, bf16[2,32,8192]{2,1,0:T(8,128)(2,1)} %fusion.3.x_ref, f32[256,128]{1,0:T(8,128)} %constant.72.clone.cos_ref, f32[256,128]{1,0:T(8,128)} %constant.73.clone.sin_ref, f32[8,128]{1,0:T(8,128)} %constant.74.clone.frequency_ref, ...), custom_call_target="tpu_custom_call" | custom-call | tf_op jit(solution)/shard_map/layer/pallas_call | solution.py:489
  126.8 3.3 %copy.18 = bf16[32,2,8192]{2,1,0:T(2,128)(2,1)} copy(bf16[32,2,8192]{2,0,1:T(8,128)(2,1)} %bitcast.13) | data formatting | bytes 2097152 | tf_op jit(solution)/shard_map/transpose | solution.py:575
  (6 shorter events, 0.1 us)

commit v4 on v3

--- a/solution.py
+++ b/solution.py
@@ -13,7 +13,7 @@
 norm_eps = 1e-05
 masked = -1e30
 log2e = 1.4426950408889634
-VMEM_LIMIT = 62 << 20
+VMEM_LIMIT = 49 << 20
 MESH = pl.DeviceIdType.MESH
 
 
@@ -28,7 +28,10 @@
     barrier = pltpu.get_barrier_semaphore()
     for device in devices:
         pl.semaphore_signal(barrier, inc=1, device_id=device, device_id_type=MESH)
-    pl.semaphore_wait(barrier, len(devices))
+
+
+def await_greetings(devices):
+    pl.semaphore_wait(pltpu.get_barrier_semaphore(), len(devices))
 
 
 def remote(source, target, sems, index, device):
@@ -43,18 +46,75 @@
 
 
 TO_RIGHT, TO_LEFT, TO_SIB, ONWARD, SIB_LEFT, SIB_RIGHT, SIB_FAR = range(7)
+FLIP, SWAPPED, PREFIX, SPAN, KEEP = 0, 1, 2, 4, 6
 SWAP, FAR, SUM_RIGHT, SUM_LEFT = range(4)
-NEIGHBOURS, FAR_BLOCK, PRODUCT = 2, 4, 5
+NEIGHBOURS, FAR_BLOCK, PRODUCT = 1, 2, 3
 CHIP_SUM, PASS_ON, RESULT = 1, 3, 5
-ROWS_FIRST, ROWS_SECOND = 3, 7
+ROWS_FIRST, ROWS_SECOND = 1, 3
 HEAD_FIRST, HEAD_SECOND = 2, 4
+GROUP = 1
+REDUCE_LAG = 1
+
+
+def table_kernel(bits, slot_ref, prefix_ref, span_ref, table_ref):
+    d = lax.axis_index("dp")
+    mask_0 = lax.bitwise_xor(slot_ref[2 * d] // 2, d)
+    mask_1 = lax.bitwise_xor(slot_ref[2 * d + 1] // 2, d)
+    flip = lax.select(mask_0 != 1, 1, 0)
+    mask = mask_0 * flip + mask_1 * (1 - flip)
+    table_ref[FLIP] = flip
+    low = 1 << bits[1]
+    place = KEEP
+    for part, count in zip((mask // low, lax.rem(mask, low)), bits):
+        for i in range(1 << count):
+            table_ref[place] = lax.select(part == i, 1, 0)
+            place += 1
+
+    def look_up(i, carry):
+        request, prefix_0, prefix_1, span_0, span_1 = carry
+        is_0 = lax.select(slot_ref[i] == 2 * d, 1, 0)
+        is_1 = lax.select(slot_ref[i] == 2 * d + 1, 1, 0)
+        return (
+            request + i * is_0,
+            prefix_0 + prefix_ref[i] * is_0,
+            prefix_1 + prefix_ref[i] * is_1,
+            span_0 + span_ref[i] * is_0,
+            span_1 + span_ref[i] * is_1,
+        )
+
+    request, prefix_0, prefix_1, span_0, span_1 = lax.fori_loop(
+        0, slot_ref.shape[0], look_up, (jnp.int32(0),) * 5
+    )
+    swapped = lax.select(lax.bitwise_xor(request // 2, d) != 1, 1, 0)
+    table_ref[SWAPPED] = swapped
+    table_ref[PREFIX] = prefix_1 * swapped + prefix_0 * (1 - swapped)
+    table_ref[PREFIX + 1] = prefix_0 * swapped + prefix_1 * (1 - swapped)
+    table_ref[SPAN] = span_1 * swapped + span_0 * (1 - swapped)
+    table_ref[SPAN + 1] = span_0 * swapped + span_1 * (1 - swapped)
+
+
+def dp_stage_bits():
+    bits = lax.axis_size("dp").bit_length() - 1
+    return bits - bits // 2, bits // 2
+
+
+def requests_table(slots, prefix, span):
+    bits = dp_stage_bits()
+    smem = pl.BlockSpec(memory_space=pltpu.SMEM)
+    return pl.pallas_call(
+        functools.partial(table_kernel, bits),
+        out_shape=jax.ShapeDtypeStruct((KEEP + sum(1 << b for b in bits),), jnp.int32),
+        in_specs=[smem] * 3,
+        out_specs=smem,
+        name="requests_table",
+    )(slots, prefix, span)
 
 
 def layer_kernel(
-    plan, flags_ref, lengths_ref, x_ref, cos_ref, sin_ref, frequency_ref,
+    plan, table_ref, x_ref, cos_ref, sin_ref, frequency_ref,
     wq_ref, wk_ref, wv_ref, wo_ref, ck_ref, cv_ref, out_ref,
     rows, ordered, hop, hopped, weights, weights_out, cache_k, cache_v, total, packed, heads,
-    back, backed, home, mine, swap_out, swap_in, far_out, far_in, sum_out, sum_in,
+    back, backed, home, swap_in, far_in, sum_in,
     local_sem, near_sem, hop_sem, gather_sem, near_back_sem, back_sem, reduce_sem,
 ):
     chunks, stage_bits, q_heads = plan
@@ -94,8 +154,13 @@
     def columns(k):
         return pl.ds(pl.multiple_of(k * width, width), width)
 
+    groups = q_heads // GROUP
+
     def head_columns(h):
         return pl.ds(pl.multiple_of(h * HD, HD), HD)
+
+    def group_columns(g):
+        return pl.ds(pl.multiple_of(g * GROUP * HD, GROUP * HD), GROUP * HD)
 
     def near(k):
         return remote(
@@ -122,36 +187,42 @@
 
     def near_back(h):
         return remote(
-            heads.at[0, :, head_columns(h)], home.at[0, :, head_columns(h)],
+            heads.at[0, :, group_columns(h)], home.at[0, :, group_columns(h)],
             near_back_sem, (h,), flipped(1),
         )
 
     def back_source(s, h):
-        return heads.at[1, :, head_columns(h)] if s == 0 else backed.at[h]
+        return heads.at[1, :, group_columns(h)] if s == 0 else backed.at[h]
 
     def backs(s, i, h):
         return remote(
             back_source(s, h), back.at[s, i, h], back_sem, (s, i, h), flipped(stage_masks[s][i])
         )
 
+    def kept(r, place):
+        return rows.at[r // chunks, lax.rem(r, chunks), place, :]
+
     def swap(r):
-        return remote(swap_out.at[r], swap_in.at[r], reduce_sem, (SWAP, r), across(sib))
+        return remote(
+            kept(r, pl.ds(span_rows // 2, span_rows // 2)), swap_in.at[r],
+            reduce_sem, (SWAP, r), across(sib),
+        )
 
     def far_sum(r):
         odd = lax.rem(r, 2)
         return remote(
-            far_out.at[r], far_in.at[r], reduce_sem, (FAR, r),
+            kept(r, at(z_far)), far_in.at[r], reduce_sem, (FAR, r),
             across(right * (1 - odd) + left * odd),
         )
 
     def sum_right(r):
         return remote(
-            sum_out.at[r, 0], sum_in.at[r, 0], reduce_sem, (SUM_RIGHT, r), across(right)
+            swap_in.at[r, pl.ds(0, block)], sum_in.at[r, 0], reduce_sem, (SUM_RIGHT, r), across(right)
         )
 
     def sum_left(r):
         return remote(
-            sum_out.at[r, 1], sum_in.at[r, 1], reduce_sem, (SUM_LEFT, r), across(left)
+            swap_in.at[r, pl.ds(block, block)], sum_in.at[r, 1], reduce_sem, (SUM_LEFT, r), across(left)
         )
 
     def weight_copy(index):
@@ -171,20 +242,22 @@
         pltpu.make_async_copy(cv_ref, cache_v, local_sem.at[4]),
     )
 
-    greet(
-        [across(right), across(left), across(sib)]
-        + [flipped(m) for masks in stage_masks for m in masks]
-    )
+    devices = [across(right), across(left), across(sib)]
+    devices += [flipped(m) for masks in stage_masks for m in masks]
+    greet(devices)
+
+    def flag(index):
+        return table_ref[index].astype(f32)
 
     def flip_flags():
-        return flags_ref[0], 1.0 - flags_ref[0]
+        return flag(FLIP), 1.0 - flag(FLIP)
 
     def swap_flags():
-        return flags_ref[1], 1.0 - flags_ref[1]
+        return flag(SWAPPED), 1.0 - flag(SWAPPED)
 
     def keep(s):
-        first = 2 + s * (1 << stage_bits[0])
-        return tuple(flags_ref[first + i] for i in range(1 << stage_bits[s]))
+        first = KEEP + s * (1 << stage_bits[0])
+        return tuple(flag(first + i) for i in range(1 << stage_bits[s]))
 
     def mix(parts, flags):
         value = parts[0].astype(f32) * flags[0]
@@ -192,29 +265,36 @@
             value = value + part.astype(f32) * flag
         return value.astype(bf16)
 
+    for copy in cache_copies:
+        copy.start()
+
     def order_rows(k, carry):
         first, second = x_ref[0, :, columns(k)], x_ref[1, :, columns(k)]
         ordered[0, k] = mix((second, first), flip_flags())
+        ordered[1, k] = mix((first, second), flip_flags())
+        return carry
+
+    lax.fori_loop(0, chunks, order_rows, 0)
+    total[...] = jnp.zeros_like(total)
+    await_greetings(devices)
+
+    def send_rows(k, carry):
         near(k).start()
-        ordered[1, k] = mix((first, second), flip_flags())
         for i in range(len(stage_masks[0])):
             hops(0, i, k).start()
         return carry
 
-    lax.fori_loop(0, chunks, order_rows, 0)
+    lax.fori_loop(0, chunks, send_rows, 0)
     for index in range(3):
         weight_copy(index).start()
-    for copy in cache_copies:
-        copy.start()
     for j in range(chunks):
         out_copy(j).start()
-    total[...] = jnp.zeros_like(total)
 
     sib_of = 1 - 2 * core
     attend_near = chunks + PRODUCT
     attend_other = total_chunks + PRODUCT
-    reduce_near = attend_near + q_heads + 1
-    reduce_other = max(attend_other + q_heads + HEAD_SECOND, reduce_near + chunks)
+    reduce_near = attend_near + groups + REDUCE_LAG
+    reduce_other = max(attend_other + groups + HEAD_SECOND, reduce_near + chunks)
     last = reduce_other + chunks + RESULT
     contract = (((1,), (1,)), ((), ()))
 
@@ -288,8 +368,8 @@
             odd = lax.rem(r, 2).astype(f32)
             far_sum(r).wait_recv()
             passed = far_in[r].astype(f32)
-            sum_out[r, 0] = (mine[r, z_right].astype(f32) + passed * (1.0 - odd)).astype(bf16)
-            sum_out[r, 1] = (mine[r, z_left].astype(f32) + passed * odd).astype(bf16)
+            swap_in[r, pl.ds(0, block)] = (kept(r, at(z_right))[...].astype(f32) + passed * (1.0 - odd)).astype(bf16)
+            swap_in[r, pl.ds(block, block)] = (kept(r, at(z_left))[...].astype(f32) + passed * odd).astype(bf16)
             sum_right(r).start()
             sum_left(r).start()
 
@@ -298,9 +378,8 @@
         @pl.when(on)
         def _():
             swap(r).wait_recv()
-            value = mine[r].astype(f32) + swap_in[r].astype(f32)
-            mine[r] = value.astype(bf16)
-            far_out[r] = mine[r, z_far]
+            own = kept(r, pl.ds(0, span_rows // 2))
+            own[...] = (own[...].astype(f32) + swap_in[r].astype(f32)).astype(bf16)
             far_sum(r).start()
 
         r, on = reduce_index(tick)
@@ -311,8 +390,8 @@
 
             @pl.when(r == 0)
             def _():
-                for h in range(q_heads):
-                    near_back(h).wait_recv()
+                for g in range(groups):
+                    near_back(g).wait_recv()
 
             @pl.when(r < chunks)
             def _():
@@ -320,8 +399,19 @@
 
             part = jnp.dot(home[p], weights_out[j], preferred_element_type=f32)
             part = part.reshape(chips, 2, block, width)
-            mine[r] = jnp.where(core == 0, part[:, 0], part[:, 1]).astype(bf16)
-            swap_out[r] = jnp.where(core == 0, part[:, 1], part[:, 0]).astype(bf16)
+            gather(TO_RIGHT, r, t, right).wait_send()
+            gather(TO_LEFT, r, t, left).wait_send()
+            gather(TO_SIB, r, t, sib).wait_send()
+            onward(r).wait_send()
+            gather(SIB_LEFT, r, left, sib).wait_send()
+            gather(SIB_RIGHT, r, right, sib).wait_send()
+            gather(SIB_FAR, r, far, sib).wait_send()
+            own = jnp.where(core == 0, part[:, 0], part[:, 1]).astype(bf16)
+            other = jnp.where(core == 0, part[:, 1], part[:, 0]).astype(bf16)
+            kept(r, pl.ds(0, span_rows // 2))[...] = own.reshape(span_rows // 2, width)
+            kept(r, pl.ds(span_rows // 2, span_rows // 2))[...] = other.reshape(
+                span_rows // 2, width
+            )
             swap(r).start()
 
         @pl.when(within(tick - PRODUCT, 0, total_chunks))
@@ -336,7 +426,7 @@
 
             @pl.when(k == chunks - 1)
             def _():
-                prefix = lengths_ref[p]
+                prefix = table_ref[PREFIX + p]
                 angle = frequency_ref[...] * prefix.astype(f32)
                 base_cos, base_sin = jnp.cos(angle)[0:1], jnp.sin(angle)[0:1]
                 cosine = cos_ref[...] * base_cos - sin_ref[...] * base_sin
@@ -355,13 +445,13 @@
                 total[...] = jnp.zeros_like(total)
 
         @pl.when(
-            within(tick - attend_near, 0, q_heads) | within(tick - attend_other, 0, q_heads)
+            within(tick - attend_near, 0, groups) | within(tick - attend_other, 0, groups)
         )
         def _():
             late = lax.select(tick >= attend_other, 1, 0)
             p = late
-            h = tick - attend_near * (1 - late) - attend_other * late
-            prefix, span = lengths_ref[p], lengths_ref[2 + p]
+            g = tick - attend_near * (1 - late) - attend_other * late
+            prefix, span = table_ref[PREFIX + p], table_ref[SPAN + p]
             prefix_rows = cache_k.shape[1]
             keys_new = packed[p, :, pl.ds(q_width, kv_width)]
             values_new = packed[p, :, pl.ds(q_width + kv_width, kv_width)]
@@ -370,35 +460,40 @@
             row = lax.broadcasted_iota(jnp.int32, (span_rows, span_rows), 0)
             column = lax.broadcasted_iota(jnp.int32, (span_rows, span_rows), 1)
             new_bias = jnp.where((column <= row) & (column < span), 0.0, masked)
-            query = packed[p, :, head_columns(h)]
-            old = lax.dot_general(query, cache_k[p], contract, preferred_element_type=f32)
-            old = old + old_bias
-            new = lax.dot_general(query, keys_new, contract, preferred_element_type=f32)
-            new = new + new_bias
-            top = jnp.maximum(
-                jnp.max(old, axis=1, keepdims=True), jnp.max(new, axis=1, keepdims=True)
-            )
-            old = jnp.exp2(old - top)
-            new = jnp.exp2(new - top)
-            weight_sum = jnp.sum(old, axis=1, keepdims=True) + jnp.sum(
-                new, axis=1, keepdims=True
-            )
-            mixed = jnp.dot(old.astype(bf16), cache_v[p], preferred_element_type=f32)
-            mixed += jnp.dot(new.astype(bf16), values_new, preferred_element_type=f32)
-            heads[p, :, head_columns(h)] = (mixed / weight_sum).astype(bf16)
+            def one_head(i, carry):
+                h = g * GROUP + i
+                query = packed[p, :, head_columns(h)]
+                old = lax.dot_general(query, cache_k[p], contract, preferred_element_type=f32)
+                old = old + old_bias
+                new = lax.dot_general(query, keys_new, contract, preferred_element_type=f32)
+                new = new + new_bias
+                top = jnp.maximum(
+                    jnp.max(old, axis=1, keepdims=True), jnp.max(new, axis=1, keepdims=True)
+                )
+                old = jnp.exp2(old - top)
+                new = jnp.exp2(new - top)
+                weight_sum = jnp.sum(old, axis=1, keepdims=True) + jnp.sum(
+                    new, axis=1, keepdims=True
+                )
+                mixed = jnp.dot(old.astype(bf16), cache_v[p], preferred_element_type=f32)
+                mixed += jnp.dot(new.astype(bf16), values_new, preferred_element_type=f32)
+                heads[p, :, head_columns(h)] = (mixed / weight_sum).astype(bf16)
+                return carry
+
+            lax.fori_loop(0, GROUP, one_head, 0)
 
             @pl.when(p == 0)
             def _():
-                near_back(h).start()
+                near_back(g).start()
 
             @pl.when(p == 1)
             def _():
                 for i in range(len(stage_masks[0])):
-                    backs(0, i, h).start()
+                    backs(0, i, g).start()
 
         for s, lag in enumerate((HEAD_FIRST, HEAD_SECOND)):
 
-            @pl.when(within(tick - attend_other - lag, 0, q_heads))
+            @pl.when(within(tick - attend_other - lag, 0, groups))
             def _(s=s, h=tick - attend_other - lag):
                 found = [back_source(s, h)[...]]
                 for i in range(len(stage_masks[s])):
@@ -410,7 +505,7 @@
                     for i in range(len(stage_masks[1])):
                         backs(1, i, h).start()
                 else:
-                    home[1, :, head_columns(h)] = value
+                    home[1, :, group_columns(h)] = value
 
         r, on = reduce_index(tick - RESULT)
 
@@ -420,7 +515,7 @@
             sum_right(r).wait_recv()
             sum_left(r).wait_recv()
             value = (
-                mine[r, z].astype(f32) + sum_in[r, 0].astype(f32) + sum_in[r, 1].astype(f32)
+                kept(r, at(z))[...].astype(f32) + sum_in[r, 0].astype(f32) + sum_in[r, 1].astype(f32)
             ).astype(bf16)
 
             @pl.when(p == 0)
@@ -444,14 +539,7 @@
                 hops(s, i, k).wait_send()
         return carry
 
-    def drain_blocks(q, carry):
-        gather(TO_RIGHT, q, t, right).wait_send()
-        gather(TO_LEFT, q, t, left).wait_send()
-        gather(TO_SIB, q, t, sib).wait_send()
-        onward(q).wait_send()
-        gather(SIB_LEFT, q, left, sib).wait_send()
-        gather(SIB_RIGHT, q, right, sib).wait_send()
-        gather(SIB_FAR, q, far, sib).wait_send()
+    def drain_sums(q, carry):
         swap(q).wait_send()
         far_sum(q).wait_send()
         sum_right(q).wait_send()
@@ -466,19 +554,19 @@
         return carry
 
     lax.fori_loop(0, chunks, drain_rows, 0)
-    lax.fori_loop(0, total_chunks, drain_blocks, 0)
-    lax.fori_loop(0, q_heads, drain_heads, 0)
-
-
-def layer(flags, lengths, x, cosine, sine, frequency, wq, wk, wv, wo, cache_keys, cache_values, chunks=8):
+    lax.fori_loop(0, total_chunks, drain_sums, 0)
+    lax.fori_loop(0, groups, drain_heads, 0)
+
+
+def layer(table, x, cosine, sine, frequency, wq, wk, wv, wo, cache_keys, cache_values, chunks=4):
     packets, block, depth = x.shape
-    n, dp = lax.axis_size("tensor"), lax.axis_size("dp")
-    low_bits = (dp.bit_length() - 1) // 2
-    stage_bits = (dp.bit_length() - 1 - low_bits, low_bits)
+    n = lax.axis_size("tensor")
+    stage_bits = dp_stage_bits()
     most = max((1 << b) - 1 for b in stage_bits)
     q_width, kv_width = wq.shape[1], wk.shape[1]
     all_width = q_width + 2 * kv_width
     q_heads = q_width // HD
+    groups = q_heads // GROUP
     rows, width = block * n, depth // chunks
     bf16, f32 = jnp.bfloat16, jnp.float32
     any_space = pl.BlockSpec(memory_space=pl.ANY)
@@ -489,7 +577,7 @@
     return pl.pallas_call(
         functools.partial(layer_kernel, (chunks, stage_bits, q_heads)),
         out_shape=jax.ShapeDtypeStruct((packets, block, depth), bf16),
-        in_specs=[smem] * 2 + [vmem] * 4 + [any_space] * 6,
+        in_specs=[smem] + [vmem] * 4 + [any_space] * 6,
         out_specs=vmem,
         scratch_shapes=[
             pltpu.VMEM((packets, chunks, rows, width), bf16),
@@ -503,29 +591,25 @@
             pltpu.VMEM((rows, all_width), f32),
             pltpu.VMEM((packets, rows, all_width), bf16),
             pltpu.VMEM((packets, rows, q_width), bf16),
-            pltpu.VMEM((2, most, q_heads, rows, HD), bf16),
-            pltpu.VMEM((q_heads, rows, HD), bf16),
+            pltpu.VMEM((2, most, groups, rows, GROUP * HD), bf16),
+            pltpu.VMEM((groups, rows, GROUP * HD), bf16),
             pltpu.VMEM((packets, rows, q_width), bf16),
-            pltpu.VMEM((steps, n // 2, block, width), bf16),
-            pltpu.VMEM((steps, n // 2, block, width), bf16),
-            pltpu.VMEM((steps, n // 2, block, width), bf16),
+            pltpu.VMEM((steps, rows // 2, width), bf16),
             pltpu.VMEM((steps, block, width), bf16),
-            pltpu.VMEM((steps, block, width), bf16),
-            pltpu.VMEM((steps, 2, block, width), bf16),
             pltpu.VMEM((steps, 2, block, width), bf16),
             dma((5 + chunks,)),
             dma((2, chunks)),
             dma((2, 2, most, chunks)),
             dma((2, 7, steps)),
-            dma((2, q_heads)),
-            dma((2, 2, most, q_heads)),
+            dma((2, groups)),
+            dma((2, 2, most, groups)),
             dma((2, 4, steps)),
         ],
         compiler_params=pltpu.CompilerParams(
             collective_id=0, has_side_effects=True, vmem_limit_bytes=VMEM_LIMIT
         ),
         name="layer",
-    )(flags, lengths, x, cosine, sine, frequency, wq, wk, wv, wo, cache_keys, cache_values)
+    )(table, x, cosine, sine, frequency, wq, wk, wv, wo, cache_keys, cache_values)
 
 
 def local(
@@ -533,32 +617,6 @@
     slot_of_request, span_length, prefix_length,
 ):
     span_rows = hidden_rows.shape[0] * lax.axis_size("tensor")
-    per_device = hidden_rows.shape[1]
-    data_index = lax.axis_index("dp")
-    low = 1 << ((lax.axis_size("dp").bit_length() - 1) // 2)
-    high = lax.axis_size("dp") // low
-    ids = jnp.arange(per_device, dtype=jnp.int32) + data_index * per_device
-    requests = jnp.arange(slot_of_request.shape[0], dtype=jnp.int32)
-    mine = requests[None, :] == ids[:, None]
-    masks = jnp.bitwise_xor(
-        jnp.sum(jnp.where(mine, slot_of_request[None, :], 0), axis=1) // per_device, data_index
-    )
-    flip = masks[0] != 1
-    mask = jnp.where(flip, masks[0], masks[1])
-    match = slot_of_request[None, :] == ids[:, None]
-    near = jnp.bitwise_xor(requests // per_device, data_index) == 1
-    swapped = ~jnp.any(match[0] & near)
-    packet = jnp.stack([jnp.where(swapped, match[1], match[0]), jnp.where(swapped, match[0], match[1])])
-    lengths = jnp.sum(
-        jnp.where(packet[None], jnp.stack([prefix_length, span_length])[:, None, :], 0), axis=-1
-    ).reshape(-1)
-    flags = jnp.concatenate(
-        [
-            flip[None], swapped[None],
-            mask // low == jnp.arange(high, dtype=jnp.int32),
-            mask % low == jnp.arange(low, dtype=jnp.int32),
-        ]
-    ).astype(jnp.float32)
     floats = hidden_rows.astype(jnp.float32)
     normed = (
         floats * lax.rsqrt(jnp.mean(floats * floats, axis=-1, keepdims=True) + norm_eps) * norm_gain
@@ -567,7 +625,8 @@
     frequency = np.concatenate([half, half])
     angles = np.arange(span_rows, dtype=np.float64)[:, None] * frequency
     result = layer(
-        flags, lengths, jnp.transpose(normed, (1, 0, 2)),
+        requests_table(slot_of_request, prefix_length, span_length),
+        jnp.transpose(normed, (1, 0, 2)),
         jnp.asarray(np.cos(angles), jnp.float32), jnp.asarray(np.sin(angles), jnp.float32),
         jnp.asarray(np.broadcast_to(frequency, (8, HD)), jnp.float32),
         w_query, w_key, w_value, w_out, cache_keys, cache_values,

time: 130 us -> 119 us (0.915)
  other arithmetic: 9 us -> 4.29 us
  between operations: 2.63 us -> 0.1 us
  local copies, waits for them, and re-layouts: 4.47 us -> 2.08 us
  Pallas kernels: 114 us -> 112 us
    pallas_call x1, Pallas kernels: 114 us -> 110 us  [layer(): pl.pallas_call(functools.partial(layer_kernel, (chunks, stage_bits, q_hea...]
    pallas_call x0 -> x1, Pallas kernels: none -> 1.85 us  [requests_table(): pl.pallas_call(functools.partial(table_kernel, bits), out_shape=jax.Shape...]
where the time goes in v4:
time: 119 us; the launch traced here: 118 us
  Pallas kernels  112 us (94%)
  other arithmetic  4.29 us (4%)
  local copies, waits for them, and re-layouts  2.08 us (2%)
    pallas_call x1, Pallas kernels, layer(): pl.pallas_call(functools.partial(layer_kernel, (chunks, stage_bits, q_hea...  110 us
    reduce_sum x1, other arithmetic, local(): jnp.mean(floats * floats, axis=-1, keepdims=True) + norm_eps  2.4 us

profile of v4, /device:TPU:1, one launch (start us, length us, event | category | flops | bytes accessed | tf_op | source)
XLA Modules:
  0.0 118.4 jit_solution(9743393530309588948)
XLA Ops:
  0.0 0.0 copy-start.4
  0.0 0.0 copy-start.2
  0.0 0.0 copy-start.3
  0.0 0.0 copy-start.1
  0.0 0.0 copy-start
  0.0 1.9 %requests_table.1.table_ref = s32[14]{0:T(128)} custom-call(s32[32]{0:T(128)} %slot_ref.1, s32[32]{0:T(128)} %prefix_ref.1, s32[32]{0:T(128)} %span_ref.1), custom_call_target="tpu_custom_call" | custom-call | tf_op jit(solution)/shard_map/requests_table/pallas_call | solution.py:104
  1.9 0.0 copy-start.5
  1.9 2.4 %fusion = f32[32,2]{0,1:T(2,128)S(1)} fusion(bf16[32,2,8192]{2,1,0:T(2,128)(2,1)} %param.14), kind=kLoop, calls=%fused_computation.2 | loop fusion | flops 1572800 | bytes 1048832 | tf_op jit(solution)/shard_map/reduce_sum | solution.py:622
  4.3 1.9 %fusion.3.x_ref = bf16[2,32,8192]{2,1,0:T(8,128)(2,1)S(1)} fusion(f32[8192]{0:T(1024)} %param.15, f32[32,2]{0,1:T(2,128)S(1)} %add_rsqrt_fusion, bf16[32,2,8192]{2,1,0:T(2,128)(2,1)} %param.14), kind=kLoop, calls=%fused_computation.5 | loop fusion | flops 2097152 | bytes 2130176 | tf_op jit(solution)/shard_map/transpose | solution.py:629
  6.2 0.0 copy-done.4
  6.2 0.0 copy-done.2
  6.2 0.0 copy-done.3
  6.2 0.0 copy-done.1
  6.2 0.0 copy-done
  6.2 0.0 copy-done.5
  6.3 110.1 %layer.1 = bf16[2,32,8192]{2,1,0:T(8,128)(2,1)S(1)} custom-call(s32[14]{0:T(128)S(1)} %copy-done.5, bf16[2,32,8192]{2,1,0:T(8,128)(2,1)S(1)} %fusion.3.x_ref, f32[256,128]{1,0:T(8,128)S(1)} %copy-done.3, f32[256,128]{1,0:T(8,128)S(1)} %copy-done.2, f32[8,128]{1,0:T(8,128)S(1)} %copy-done.4, bf16[8192,512]{1,0:T(8,128)(2,1)} %wq_ref.1, ...), custom_call_target="tpu_custom_call" | custom-call | tf_op jit(solution)/shard_map/layer/pallas_call | solution.py:577
  116.4 2.1 %copy.16 = bf16[32,2,8192]{2,1,0:T(2,128)(2,1)} copy(bf16[32,2,8192]{2,0,1:T(8,128)(2,1)S(1)} %bitcast.3) | data formatting | bytes 2097152 | tf_op jit(solution)/shard_map/transpose | solution.py:634
  (1 shorter events, 0.0 us)
Async XLA Ops:
  0.0 6.2 %copy-start.4 = (f32[8,128]{1,0:T(8,128)S(1)}, f32[8,128]{1,0:T(8,128)}, u32[]{:S(2)}) copy-start(f32[8,128]{1,0:T(8,128)} %constant.15.clone.frequency_ref) | copy-start | bytes 12292
  0.0 6.2 %copy-start.2 = (f32[256,128]{1,0:T(8,128)S(1)}, f32[256,128]{1,0:T(8,128)}, u32[]{:S(2)}) copy-start(f32[256,128]{1,0:T(8,128)} %constant.14.clone.sin_ref) | copy-start | bytes 393220
  0.0 6.2 %copy-start.3 = (f32[256,128]{1,0:T(8,128)S(1)}, f32[256,128]{1,0:T(8,128)}, u32[]{:S(2)}) copy-start(f32[256,128]{1,0:T(8,128)} %constant.13.clone.cos_ref) | copy-start | bytes 393220
  0.0 6.2 %copy-start.1 = (bf16[2,2048,128]{2,1,0:T(8,128)(2,1)S(1)}, bf16[2,2048,128]{2,1,0:T(8,128)(2,1)}, u32[]{:S(2)}) copy-start(bf16[2,2048,128]{2,1,0:T(8,128)(2,1)} %cv_ref.1) | copy-start | bytes 3145732
  0.0 6.2 %copy-start = (bf16[2,2048,128]{2,1,0:T(8,128)(2,1)S(1)}, bf16[2,2048,128]{2,1,0:T(8,128)(2,1)}, u32[]{:S(2)}) copy-start(bf16[2,2048,128]{2,1,0:T(8,128)(2,1)} %ck_ref.1) | copy-start | bytes 3145732
  1.9 4.4 %copy-start.5 = (s32[14]{0:T(128)S(1)}, s32[14]{0:T(128)}, u32[]{:S(2)}) copy-start(s32[14]{0:T(128)} %requests_table.1.table_ref) | copy-start | bytes 172

commit v5 on v4

--- a/solution.py
+++ b/solution.py
@@ -48,12 +48,12 @@
 TO_RIGHT, TO_LEFT, TO_SIB, ONWARD, SIB_LEFT, SIB_RIGHT, SIB_FAR = range(7)
 FLIP, SWAPPED, PREFIX, SPAN, KEEP = 0, 1, 2, 4, 6
 SWAP, FAR, SUM_RIGHT, SUM_LEFT = range(4)
-NEIGHBOURS, FAR_BLOCK, PRODUCT = 1, 2, 3
+NEIGHBOURS, FAR_BLOCK, PRODUCT = 2, 4, 5
 CHIP_SUM, PASS_ON, RESULT = 1, 3, 5
-ROWS_FIRST, ROWS_SECOND = 1, 3
+ROWS_FIRST, ROWS_SECOND = 3, 7
 HEAD_FIRST, HEAD_SECOND = 2, 4
 GROUP = 1
-REDUCE_LAG = 1
+REDUCE_LAG = 4
 
 
 def table_kernel(bits, slot_ref, prefix_ref, span_ref, table_ref):
@@ -360,18 +360,6 @@
                 cache[1] = mix((first, second), swap_flags())
             for index in range(3):
                 weight_copy(index).wait()
-
-        r, on = reduce_index(tick - PASS_ON)
-
-        @pl.when(on)
-        def _():
-            odd = lax.rem(r, 2).astype(f32)
-            far_sum(r).wait_recv()
-            passed = far_in[r].astype(f32)
-            swap_in[r, pl.ds(0, block)] = (kept(r, at(z_right))[...].astype(f32) + passed * (1.0 - odd)).astype(bf16)
-            swap_in[r, pl.ds(block, block)] = (kept(r, at(z_left))[...].astype(f32) + passed * odd).astype(bf16)
-            sum_right(r).start()
-            sum_left(r).start()
 
         r, on = reduce_index(tick - CHIP_SUM)
 
@@ -507,6 +495,18 @@
                 else:
                     home[1, :, group_columns(h)] = value
 
+        r, on = reduce_index(tick - PASS_ON)
+
+        @pl.when(on)
+        def _():
+            odd = lax.rem(r, 2).astype(f32)
+            far_sum(r).wait_recv()
+            passed = far_in[r].astype(f32)
+            swap_in[r, pl.ds(0, block)] = (kept(r, at(z_right))[...].astype(f32) + passed * (1.0 - odd)).astype(bf16)
+            swap_in[r, pl.ds(block, block)] = (kept(r, at(z_left))[...].astype(f32) + passed * odd).astype(bf16)
+            sum_right(r).start()
+            sum_left(r).start()
+
         r, on = reduce_index(tick - RESULT)
 
         @pl.when(on)
@@ -558,7 +558,7 @@
     lax.fori_loop(0, groups, drain_heads, 0)
 
 
-def layer(table, x, cosine, sine, frequency, wq, wk, wv, wo, cache_keys, cache_values, chunks=4):
+def layer(table, x, cosine, sine, frequency, wq, wk, wv, wo, cache_keys, cache_values, chunks=8):
     packets, block, depth = x.shape
     n = lax.axis_size("tensor")
     stage_bits = dp_stage_bits()

time: 119 us -> 117 us (0.983)
  Pallas kernels: 112 us -> 110 us
    pallas_call x1, Pallas kernels: 110 us -> 108 us  [layer(): pl.pallas_call(functools.partial(layer_kernel, (chunks, stage_bits, q_hea...]
where the time goes in v5:
time: 117 us; the launch traced here: 116 us
  Pallas kernels  110 us (94%)
  other arithmetic  4.29 us (4%)
  local copies, waits for them, and re-layouts  2.08 us (2%)
    pallas_call x1, Pallas kernels, layer(): pl.pallas_call(functools.partial(layer_kernel, (chunks, stage_bits, q_hea...  108 us
    reduce_sum x1, other arithmetic, local(): jnp.mean(floats * floats, axis=-1, keepdims=True) + norm_eps  2.4 us

profile of v5, /device:TPU:1, one launch (start us, length us, event | category | flops | bytes accessed | tf_op | source)
XLA Modules:
  0.0 116.3 jit_solution(9363825572271658713)
XLA Ops:
  0.0 0.0 copy-start.4
  0.0 0.0 copy-start.2
  0.0 0.0 copy-start.3
  0.0 0.0 copy-start.1
  0.0 0.0 copy-start
  0.0 1.9 %requests_table.1.table_ref = s32[14]{0:T(128)} custom-call(s32[32]{0:T(128)} %slot_ref.1, s32[32]{0:T(128)} %prefix_ref.1, s32[32]{0:T(128)} %span_ref.1), custom_call_target="tpu_custom_call" | custom-call | tf_op jit(solution)/shard_map/requests_table/pallas_call | solution.py:104
  1.9 0.0 copy-start.5
  1.9 2.4 %fusion = f32[32,2]{0,1:T(2,128)S(1)} fusion(bf16[32,2,8192]{2,1,0:T(2,128)(2,1)} %param.14), kind=kLoop, calls=%fused_computation.2 | loop fusion | flops 1572800 | bytes 1048832 | tf_op jit(solution)/shard_map/reduce_sum | solution.py:622
  4.3 1.9 %fusion.3.x_ref = bf16[2,32,8192]{2,1,0:T(8,128)(2,1)S(1)} fusion(f32[8192]{0:T(1024)} %param.15, f32[32,2]{0,1:T(2,128)S(1)} %add_rsqrt_fusion, bf16[32,2,8192]{2,1,0:T(2,128)(2,1)} %param.14), kind=kLoop, calls=%fused_computation.5 | loop fusion | flops 2097152 | bytes 2130176 | tf_op jit(solution)/shard_map/transpose | solution.py:629
  6.2 0.0 copy-done.4
  6.2 0.0 copy-done.2
  6.2 0.0 copy-done.3
  6.2 0.0 copy-done.1
  6.2 0.0 copy-done
  6.2 0.0 copy-done.5
  6.3 108.0 %layer.1 = bf16[2,32,8192]{2,1,0:T(8,128)(2,1)S(1)} custom-call(s32[14]{0:T(128)S(1)} %copy-done.5, bf16[2,32,8192]{2,1,0:T(8,128)(2,1)S(1)} %fusion.3.x_ref, f32[256,128]{1,0:T(8,128)S(1)} %copy-done.3, f32[256,128]{1,0:T(8,128)S(1)} %copy-done.2, f32[8,128]{1,0:T(8,128)S(1)} %copy-done.4, bf16[8192,512]{1,0:T(8,128)(2,1)} %wq_ref.1, ...), custom_call_target="tpu_custom_call" | custom-call | tf_op jit(solution)/shard_map/layer/pallas_call | solution.py:577
  114.3 2.1 %copy.16 = bf16[32,2,8192]{2,1,0:T(2,128)(2,1)} copy(bf16[32,2,8192]{2,0,1:T(8,128)(2,1)S(1)} %bitcast.3) | data formatting | bytes 2097152 | tf_op jit(solution)/shard_map/transpose | solution.py:634
  (1 shorter events, 0.0 us)
Async XLA Ops:
  0.0 6.2 %copy-start.4 = (f32[8,128]{1,0:T(8,128)S(1)}, f32[8,128]{1,0:T(8,128)}, u32[]{:S(2)}) copy-start(f32[8,128]{1,0:T(8,128)} %constant.15.clone.frequency_ref) | copy-start | bytes 12292
  0.0 6.2 %copy-start.2 = (f32[256,128]{1,0:T(8,128)S(1)}, f32[256,128]{1,0:T(8,128)}, u32[]{:S(2)}) copy-start(f32[256,128]{1,0:T(8,128)} %constant.14.clone.sin_ref) | copy-start | bytes 393220
  0.0 6.2 %copy-start.3 = (f32[256,128]{1,0:T(8,128)S(1)}, f32[256,128]{1,0:T(8,128)}, u32[]{:S(2)}) copy-start(f32[256,128]{1,0:T(8,128)} %constant.13.clone.cos_ref) | copy-start | bytes 393220
  0.0 6.2 %copy-start.1 = (bf16[2,2048,128]{2,1,0:T(8,128)(2,1)S(1)}, bf16[2,2048,128]{2,1,0:T(8,128)(2,1)}, u32[]{:S(2)}) copy-start(bf16[2,2048,128]{2,1,0:T(8,128)(2,1)} %cv_ref.1) | copy-start | bytes 3145732
  0.0 6.2 %copy-start = (bf16[2,2048,128]{2,1,0:T(8,128)(2,1)S(1)}, bf16[2,2048,128]{2,1,0:T(8,128)(2,1)}, u32[]{:S(2)}) copy-start(bf16[2,2048,128]{2,1,0:T(8,128)(2,1)} %ck_ref.1) | copy-start | bytes 3145732
  1.9 4.4 %copy-start.5 = (s32[14]{0:T(128)S(1)}, s32[14]{0:T(128)}, u32[]{:S(2)}) copy-start(s32[14]{0:T(128)} %requests_table.1.table_ref) | copy-start | bytes 172

commit v6 on v5

--- a/solution.py
+++ b/solution.py
@@ -49,7 +49,7 @@
 FLIP, SWAPPED, PREFIX, SPAN, KEEP = 0, 1, 2, 4, 6
 SWAP, FAR, SUM_RIGHT, SUM_LEFT = range(4)
 NEIGHBOURS, FAR_BLOCK, PRODUCT = 2, 4, 5
-CHIP_SUM, PASS_ON, RESULT = 1, 3, 5
+CHIP_SUM, PASS_ON, RESULT = 1, 3, 6
 ROWS_FIRST, ROWS_SECOND = 3, 7
 HEAD_FIRST, HEAD_SECOND = 2, 4
 GROUP = 1

time: 117 us -> 117 us (level)
  no operation moved by 1% of the time
where the time goes in v6:
time: 117 us; the launch traced here: 116 us
  Pallas kernels  110 us (94%)
  other arithmetic  4.29 us (4%)
  local copies, waits for them, and re-layouts  2.08 us (2%)
    pallas_call x1, Pallas kernels, layer(): pl.pallas_call(functools.partial(layer_kernel, (chunks, stage_bits, q_hea...  108 us
    reduce_sum x1, other arithmetic, local(): jnp.mean(floats * floats, axis=-1, keepdims=True) + norm_eps  2.4 us

profile of v6, /device:TPU:1, one launch (start us, length us, event | category | flops | bytes accessed | tf_op | source)
XLA Modules:
  0.0 116.3 jit_solution(17942171648519104900)
XLA Ops:
  0.0 0.0 copy-start.4
  0.0 0.0 copy-start.2
  0.0 0.0 copy-start.3
  0.0 0.0 copy-start.1
  0.0 0.0 copy-start
  0.0 1.9 %requests_table.1.table_ref = s32[14]{0:T(128)} custom-call(s32[32]{0:T(128)} %slot_ref.1, s32[32]{0:T(128)} %prefix_ref.1, s32[32]{0:T(128)} %span_ref.1), custom_call_target="tpu_custom_call" | custom-call | tf_op jit(solution)/shard_map/requests_table/pallas_call | solution.py:104
  1.9 0.0 copy-start.5
  1.9 2.4 %fusion = f32[32,2]{0,1:T(2,128)S(1)} fusion(bf16[32,2,8192]{2,1,0:T(2,128)(2,1)} %param.14), kind=kLoop, calls=%fused_computation.2 | loop fusion | flops 1572800 | bytes 1048832 | tf_op jit(solution)/shard_map/reduce_sum | solution.py:622
  4.3 1.9 %fusion.3.x_ref = bf16[2,32,8192]{2,1,0:T(8,128)(2,1)S(1)} fusion(f32[8192]{0:T(1024)} %param.15, f32[32,2]{0,1:T(2,128)S(1)} %add_rsqrt_fusion, bf16[32,2,8192]{2,1,0:T(2,128)(2,1)} %param.14), kind=kLoop, calls=%fused_computation.5 | loop fusion | flops 2097152 | bytes 2130176 | tf_op jit(solution)/shard_map/transpose | solution.py:629
  6.2 0.0 copy-done.4
  6.2 0.0 copy-done.2
  6.2 0.0 copy-done.3
  6.2 0.0 copy-done.1
  6.2 0.0 copy-done
  6.2 0.0 copy-done.5
  6.3 108.0 %layer.1 = bf16[2,32,8192]{2,1,0:T(8,128)(2,1)S(1)} custom-call(s32[14]{0:T(128)S(1)} %copy-done.5, bf16[2,32,8192]{2,1,0:T(8,128)(2,1)S(1)} %fusion.3.x_ref, f32[256,128]{1,0:T(8,128)S(1)} %copy-done.3, f32[256,128]{1,0:T(8,128)S(1)} %copy-done.2, f32[8,128]{1,0:T(8,128)S(1)} %copy-done.4, bf16[8192,512]{1,0:T(8,128)(2,1)} %wq_ref.1, ...), custom_call_target="tpu_custom_call" | custom-call | tf_op jit(solution)/shard_map/layer/pallas_call | solution.py:577
  114.3 2.1 %copy.16 = bf16[32,2,8192]{2,1,0:T(2,128)(2,1)} copy(bf16[32,2,8192]{2,0,1:T(8,128)(2,1)S(1)} %bitcast.3) | data formatting | bytes 2097152 | tf_op jit(solution)/shard_map/transpose | solution.py:634
  (1 shorter events, 0.0 us)
Async XLA Ops:
  0.0 6.2 %copy-start.4 = (f32[8,128]{1,0:T(8,128)S(1)}, f32[8,128]{1,0:T(8,128)}, u32[]{:S(2)}) copy-start(f32[8,128]{1,0:T(8,128)} %constant.15.clone.frequency_ref) | copy-start | bytes 12292
  0.0 6.2 %copy-start.2 = (f32[256,128]{1,0:T(8,128)S(1)}, f32[256,128]{1,0:T(8,128)}, u32[]{:S(2)}) copy-start(f32[256,128]{1,0:T(8,128)} %constant.14.clone.sin_ref) | copy-start | bytes 393220
  0.0 6.2 %copy-start.3 = (f32[256,128]{1,0:T(8,128)S(1)}, f32[256,128]{1,0:T(8,128)}, u32[]{:S(2)}) copy-start(f32[256,128]{1,0:T(8,128)} %constant.13.clone.cos_ref) | copy-start | bytes 393220
  0.0 6.2 %copy-start.1 = (bf16[2,2048,128]{2,1,0:T(8,128)(2,1)S(1)}, bf16[2,2048,128]{2,1,0:T(8,128)(2,1)}, u32[]{:S(2)}) copy-start(bf16[2,2048,128]{2,1,0:T(8,128)(2,1)} %cv_ref.1) | copy-start | bytes 3145732
  0.0 6.2 %copy-start = (bf16[2,2048,128]{2,1,0:T(8,128)(2,1)S(1)}, bf16[2,2048,128]{2,1,0:T(8,128)(2,1)}, u32[]{:S(2)}) copy-start(bf16[2,2048,128]{2,1,0:T(8,128)(2,1)} %ck_ref.1) | copy-start | bytes 3145732
  1.9 4.4 %copy-start.5 = (s32[14]{0:T(128)S(1)}, s32[14]{0:T(128)}, u32[]{:S(2)}) copy-start(s32[14]{0:T(128)} %requests_table.1.table_ref) | copy-start | bytes 172
